TPU v7x, 512 devices: a whole 4x8x8 slice. The times are simulated.
512 devices in a mesh: fsdp: 128 (over y, z_lo, x), dp: 4 (over z_hi, core).
Axes of the slice: x: 4, y: 8, z: 8 (z_hi: 2, z_lo: 4; z = z_hi * 4 + z_lo), core: 2. Of those that a mesh axis runs over, the one named last changes fastest.
Arguments:
- candidate_layer_inputs: bfloat16 [2048, 32, 8192], P(('dp', 'fsdp')), parts along dimension 0, may hold values from -8 to 8
- candidate_loss_cotangent: bfloat16 [2048, 32, 1024], P(('dp', 'fsdp')), parts along dimension 0, may hold values from -8 to 8
- candidate_live_lengths: int32 [2048], P(('dp', 'fsdp')), parts along dimension 0, may hold values from 4 to 32, as said below
- probe_layer_inputs: bfloat16 [2048, 32, 8192], P(('dp', 'fsdp')), parts along dimension 0, may hold values from -8 to 8
- probe_loss_cotangent: bfloat16 [2048, 32, 1024], P(('dp', 'fsdp')), parts along dimension 0, may hold values from -8 to 8
- probe_live_lengths: int32 [2048], P(('dp', 'fsdp')), parts along dimension 0, may hold values from 4 to 32, as said below
- adapter_down_matrix: bfloat16 [8192, 128], P('fsdp'), may hold values from -0.0625 to 0.0625
- adapter_up_matrix: bfloat16 [1024, 128], P('fsdp'), may hold values from -0.5 to 0.5
- input_side_sketch: bfloat16 [8192, 256], P('fsdp'), may hold values from -0.0625 to 0.0625
- output_side_sketch: bfloat16 [1024, 256], P('fsdp'), may hold values from -0.1875 to 0.1875
- rank_sketch_down: bfloat16 [128, 16], replicated, may hold values from -0.5 to 0.5
- rank_sketch_up: bfloat16 [128, 16], replicated, may hold values from -0.5 to 0.5
Outputs:
- scores: float32 [2048, 512], P(('dp', 'fsdp')), parts along dimension 0
- features: bfloat16 [2048, 8192], P(('dp', 'fsdp')), parts along dimension 0
There are 4 independent parts, one for each index of `dp`. A program takes and returns all parts, laid end to end along the dimension named above; an argument that names none is the same for every part. Nothing has to cross between parts.
Inputs may be any that keep to these rules, and one draw needn't show every extreme that they name: `candidate_live_lengths`: the live positions of an example are its first that many; some example has exactly 32 live positions and some exactly 4. `probe_live_lengths`: the live positions of an example are its first that many; some example has exactly 32 live positions and some exactly 4.
All inputs are finite; a program needn't handle non-finite values.
Results may differ from a plain program's by a relative error of at most 0.0056.
Values may be sent and summed in bfloat16 or wider, within the bound.
A program may use at most 64 MiB of HBM per device.

v0:
```python
import jax
import jax.numpy as jnp
from jax import lax
from jax.sharding import Mesh
from jax.sharding import PartitionSpec as P

FSDP = ("fsdp_0", "fsdp_1", "fsdp_2")
DP_FSDP = ("dp", "fsdp_0", "fsdp_1", "fsdp_2")


eps_mean = 1e-06


def sent_to_all(value, axis):
    copies = jnp.broadcast_to(value, (lax.axis_size(axis), *value.shape))
    return lax.all_to_all(copies, axis, split_axis=0, concat_axis=0, tiled=True)


def in_order(parts, dim):
    shape = list(parts.shape[1:])
    shape[dim] *= parts.shape[0]
    return jnp.moveaxis(parts, 0, dim).reshape(shape)


def gather_axes(value, axes, dim):
    far, near = axes
    initial = sent_to_all(value, far)
    parts = jnp.swapaxes(sent_to_all(initial, near), 0, 1)
    return in_order(parts.reshape(-1, *value.shape), dim)


def side_by_side(arrays, axis, dim, along):
    widths = [a.shape[along] for a in arrays]
    both = jnp.concatenate(arrays, axis=along)
    filled = gather_axes(both, axis, dim)
    return tuple(jnp.split(filled, [sum(widths[:k]) for k in range(1, len(widths))], axis=along))


def side_by_side_2(arrays, axis, dim, along):
    both = jnp.concatenate(arrays, axis=along)
    filled, at, done = (lax.all_gather(both, axis, axis=dim, tiled=True), 0, [])
    for a in arrays:
        done.append(lax.slice_in_dim(filled, at, at + a.shape[along], axis=along))
        at += a.shape[along]
    return tuple(done)


def split_up(value, dim, count):
    before, after = (value.shape[:dim], value.shape[dim + 1 :])
    return jnp.moveaxis(value.reshape(*before, count, -1, *after), dim, 0)


def sent_and_summed(value, axis, dim):
    count = lax.axis_size(axis)
    parts = lax.all_to_all(split_up(value, dim, count), axis, 0, 0, tiled=True)
    return jnp.sum(parts, axis=0)


def sum_in_two_steps(value, axes, dim):
    far, near = axes
    own = sent_and_summed(split_up(value, dim, lax.axis_size(far)), near, dim + 1)
    return jnp.sum(lax.all_to_all(own, far, 0, 0, tiled=True), axis=0)


def live_cotangent(loss_cotangent, example_lengths):
    positions = lax.broadcasted_iota(jnp.int32, loss_cotangent.shape[:2], 1)
    live_mask = (positions < example_lengths[:, None]).astype(loss_cotangent.dtype)
    return loss_cotangent * live_mask[:, :, None]


def compute_sketch_features(
    down_total_acc,
    inward_total_acc,
    loss_cotangent,
    example_lengths,
    up_full,
    outward_full,
    rank_sketch_down,
    rank_sketch_up,
):
    examples = loss_cotangent.shape[0]
    seq_len = loss_cotangent.shape[1]
    kv_width = loss_cotangent.shape[2]
    masked_values = live_cotangent(loss_cotangent, example_lengths).reshape(
        examples * seq_len, kv_width
    )
    gradient_rowset = jnp.dot(masked_values, up_full, preferred_element_type=jnp.float32).astype(
        jnp.bfloat16
    )
    outward = jnp.dot(masked_values, outward_full, preferred_element_type=jnp.float32).astype(
        jnp.bfloat16
    )
    down_round = down_total_acc.astype(jnp.bfloat16)
    inward_round = inward_total_acc.astype(jnp.bfloat16)
    left_small = jnp.dot(
        gradient_rowset, rank_sketch_down, preferred_element_type=jnp.float32
    ).astype(jnp.bfloat16)
    right_small = jnp.dot(down_round, rank_sketch_up, preferred_element_type=jnp.float32).astype(
        jnp.bfloat16
    )
    small_cols = rank_sketch_down.shape[1]
    large_cols = inward_round.shape[1]
    grad_left = jnp.einsum(
        "esk,esp->ekp",
        left_small.reshape(examples, seq_len, small_cols),
        inward_round.reshape(examples, seq_len, large_cols),
        preferred_element_type=jnp.float32,
    )
    grad_right = jnp.einsum(
        "esk,esp->ekp",
        right_small.reshape(examples, seq_len, small_cols),
        outward.reshape(examples, seq_len, large_cols),
        preferred_element_type=jnp.float32,
    )
    joined = jnp.concatenate([grad_left, grad_right], axis=1).reshape(
        examples, 2 * small_cols * large_cols
    )
    inv_rms = lax.rsqrt(jnp.mean(joined * joined, axis=1, keepdims=True) + eps_mean)
    return (joined * inv_rms).astype(jnp.bfloat16)


def body(
    candidate_layer_inputs,
    candidate_loss_cotangent,
    candidate_live_lengths,
    probe_layer_inputs,
    probe_loss_cotangent,
    probe_live_lengths,
    adapter_down_matrix,
    adapter_up_matrix,
    input_side_sketch,
    output_side_sketch,
    rank_sketch_down,
    rank_sketch_up,
):
    model_width = candidate_layer_inputs.shape[2]
    train_flat = candidate_layer_inputs.reshape(-1, model_width)
    probe_flat = probe_layer_inputs.reshape(-1, model_width)
    up_full, outward_full = side_by_side(
        (adapter_up_matrix, output_side_sketch), (("fsdp_0", "fsdp_1"), "fsdp_2"), 0, 1
    )

    def combine_couple(shard_rows):
        return (
            jnp.dot(train_flat, shard_rows, preferred_element_type=jnp.float32),
            jnp.dot(probe_flat, shard_rows, preferred_element_type=jnp.float32),
        )

    down_rows, inward_rows = side_by_side_2((adapter_down_matrix, input_side_sketch), FSDP, 0, 1)
    new_down = combine_couple(down_rows)
    new_in = combine_couple(inward_rows)
    candidate_down_gradient = new_down[0]
    probe_down_gradient = new_down[1]
    train_in = new_in[0]
    probe_in = new_in[1]
    probe_normed = compute_sketch_features(
        probe_down_gradient,
        probe_in,
        probe_loss_cotangent,
        probe_live_lengths,
        up_full,
        outward_full,
        rank_sketch_down,
        rank_sketch_up,
    )
    train_normed = compute_sketch_features(
        candidate_down_gradient,
        train_in,
        candidate_loss_cotangent,
        candidate_live_lengths,
        up_full,
        outward_full,
        rank_sketch_down,
        rank_sketch_up,
    )
    feat_count = train_normed.shape[1]
    train_block, probe_block = (
        lax.all_to_all(train_normed, FSDP, split_axis=1, concat_axis=0, tiled=True),
        lax.all_to_all(probe_normed, FSDP, split_axis=1, concat_axis=0, tiled=True),
    )
    summed = sum_in_two_steps(
        jnp.dot(train_block, probe_block.T, preferred_element_type=jnp.float32),
        (("fsdp_0", "fsdp_1"), "fsdp_2"),
        0,
    )
    scores = summed / feat_count
    return (scores, train_normed)


def solution(mesh):
    split = Mesh(
        mesh.devices.reshape(8, 4, 4, mesh.shape["dp"]), ("fsdp_0", "fsdp_1", "fsdp_2", "dp")
    )
    return jax.shard_map(
        body,
        mesh=split,
        in_specs=(
            P(DP_FSDP, None, None),
            P(DP_FSDP, None, None),
            P(DP_FSDP),
            P(DP_FSDP, None, None),
            P(DP_FSDP, None, None),
            P(DP_FSDP),
            P(FSDP, None),
            P(FSDP, None),
            P(FSDP, None),
            P(FSDP, None),
            P(),
            P(),
        ),
        out_specs=(P(DP_FSDP, None), P(DP_FSDP, None)),
        check_vma=False,
    )
```

profile of v0, /device:TPU:8, one launch (start us, length us, event | category | flops | bytes accessed | tf_op | source)
XLA Modules:
  0.0 803.5 jit_solution(14716272603627549199)
XLA Ops:
  7.2 0.0 copy-start
  7.2 0.0 all-gather.2.cloned.1.call-start
  7.3 1.5 pad_maximum_fusion.2
  8.8 0.0 all-gather.2.cloned.1.call-update
  8.8 0.7 pad_maximum_fusion.3
  9.5 0.7 broadcast_in_dim.4
  10.2 13.1 %all-to-all-start = ((bf16[32,8,384]{2,1,0:T(8,128)(2,1)}), bf16[32,8,384]{2,1,0:T(8,128)(2,1)S(1)}, u32[]{:S(2)}, u32[]{:S(2)}) async-start(bf16[32,8,384]{2,1,0:T(8,128)(2,1)} %broadcast_in_dim.4), calls=%async_computation | async-start | bytes 393216 | tf_op jit(solution)/shard_map/all_to_all | solution.py:16
  23.4 0.7 fusion.51
  24.1 10.6 %all-to-all-done = bf16[32,8,384]{2,1,0:T(8,128)(2,1)S(1)} async-done(((bf16[32,8,384]{2,1,0:T(8,128)(2,1)}), bf16[32,8,384]{2,1,0:T(8,128)(2,1)S(1)}, u32[]{:S(2)}, u32[]{:S(2)}) %all-to-all-start) | async-done | bytes 196640 | tf_op jit(solution)/shard_map/all_to_all | solution.py:16
  34.7 1.0 broadcast_in_dim.5
  35.6 4.4 all-to-all-start.1
  40.1 0.1 fusion.52
  40.1 0.8 broadcast_multiply_fusion
  41.0 0.8 broadcast_multiply_fusion.1
  41.8 10.0 %all-to-all-done.1 = bf16[4,32,8,384]{3,2,1,0:T(8,128)(2,1)S(1)} async-done(((bf16[4,32,8,384]{3,2,1,0:T(8,128)(2,1)}), bf16[4,32,8,384]{3,2,1,0:T(8,128)(2,1)S(1)}, u32[]{:S(2)}, u32[]{:S(2)}) %all-to-all-start.1) | async-done | bytes 786464 | tf_op jit(solution)/shard_map/all_to_all | solution.py:16
  51.8 1.0 copy.36
  52.7 0.0 copy-done.6
  52.7 1.4 fusion.35
  54.1 0.1 reshape.125
  54.2 0.0 copy-done.3
  54.2 1.3 fusion.34
  55.5 0.1 reshape.132
  55.6 1.3 convolution_convert_fusion
  56.9 1.3 convolution_convert_fusion.1
  58.1 622.9 %all-gather.2.cloned.1.call-done = bf16[8192,384]{1,0:T(8,128)(2,1)} async-done(((bf16[64,384]{1,0:T(8,128)(2,1)}), bf16[8192,384]{1,0:T(8,128)(2,1)}) %all-gather.2.cloned.1.call-update) | async-done | bytes 6291472 | tf_op jit(solution)/shard_map/all_gather | solution.py:41
  681.0 0.0 copy-done.7
  681.0 3.1 fusion.28
  684.1 0.1 reshape.128
  684.2 0.0 copy-done
  684.2 2.5 fusion.31
  686.7 0.1 reshape.135
  686.8 0.1 fusion.43
  686.9 3.1 fusion.8
  690.0 0.1 fusion.45
  690.1 0.1 multiply_reduce_fusion
  690.2 0.1 fusion.47
  690.3 3.0 fusion.11
  693.3 0.1 fusion.49
  693.5 0.1 fusion.53
  693.6 0.1 reshape.130
  693.7 0.1 multiply_convert_fusion.1
  693.8 0.1 copy.63
  693.9 0.7 reshape.142
  694.6 38.9 %all-to-all-start.2 = ((bf16[128,2,128]{2,1,0:T(2,128)(2,1)}), bf16[128,2,128]{2,1,0:T(2,128)(2,1)S(1)}, u32[]{:S(2)}, u32[]{:S(2)}) async-start(bf16[128,2,128]{2,1,0:T(2,128)(2,1)} %reshape.142), calls=%async_computation.2 | async-start | bytes 131072 | tf_op jit(solution)/shard_map/all_to_all | solution.py:178
  733.6 0.1 reshape.137
  733.7 0.1 multiply_convert_fusion
  733.8 0.1 copy.62
  733.9 0.7 reshape.140
  734.6 10.5 %all-to-all-done.2 = bf16[128,2,128]{2,1,0:T(2,128)(2,1)S(1)} async-done(((bf16[128,2,128]{2,1,0:T(2,128)(2,1)}), bf16[128,2,128]{2,1,0:T(2,128)(2,1)S(1)}, u32[]{:S(2)}, u32[]{:S(2)}) %all-to-all-start.2) | async-done | bytes 65568 | tf_op jit(solution)/shard_map/all_to_all | solution.py:178
  745.2 6.4 all-to-all-start.3
  751.6 0.1 reshape.143
  751.7 11.4 %all-to-all-done.3 = bf16[128,2,128]{2,1,0:T(2,128)(2,1)S(1)} async-done(((bf16[128,2,128]{2,1,0:T(2,128)(2,1)}), bf16[128,2,128]{2,1,0:T(2,128)(2,1)S(1)}, u32[]{:S(2)}, u32[]{:S(2)}) %all-to-all-start.3) | async-done | bytes 65568 | tf_op jit(solution)/shard_map/all_to_all | solution.py:179
  763.2 0.1 reshape.141
  763.3 1.3 convolution_bitcast_fusion
  764.5 3.5 all-to-all-start.4
  768.1 0.1 copy.49
  768.2 10.8 %all-to-all-done.4 = f32[4,32,4,512]{3,1,2,0:T(8,128)S(1)} async-done(((f32[4,32,4,512]{3,1,2,0:T(8,128)}), f32[4,32,4,512]{3,1,2,0:T(8,128)S(1)}, u32[]{:S(2)}, u32[]{:S(2)}) %all-to-all-start.4) | async-done | bytes 1048608 | tf_op jit(solution)/shard_map/all_to_all | solution.py:55
  778.9 0.1 reduce_sum.38
  779.0 0.9 copy.46
  779.9 4.7 all-to-all-start.5
  784.6 0.7 multiply_convert_fusion.2
  785.4 10.6 %all-to-all-done.5 = f32[32,4,512]{2,1,0:T(4,128)S(1)} async-done(((f32[32,4,512]{2,1,0:T(4,128)}), f32[32,4,512]{2,1,0:T(4,128)S(1)}, u32[]{:S(2)}, u32[]{:S(2)}) %all-to-all-start.5) | async-done | bytes 262176 | tf_op jit(solution)/shard_map/all_to_all | solution.py:62
  795.9 0.1 reduce_sum.39
  796.0 0.6 broadcast_multiply_fusion.2
  (16 shorter events, 0.1 us)
Async XLA Ops:
  7.2 677.0 %copy-start = (bf16[4,32,8192]{2,1,0:T(8,128)(2,1)S(1)}, bf16[4,32,8192]{2,1,0:T(8,128)(2,1)}, u32[]{:S(2)}) copy-start(bf16[4,32,8192]{2,1,0:T(8,128)(2,1)} %param.15) | copy-start | bytes 6291460
  7.2 32.9 %copy-start.8 = (s32[4]{0:T(128)S(1)}, s32[4]{0:T(128)}, u32[]{:S(2)}) copy-start(s32[4]{0:T(128)} %param.17) | copy-start | bytes 52
  7.2 33.0 %copy-start.1 = (bf16[4,32,1024]{2,1,0:T(8,128)(2,1)S(1)}, bf16[4,32,1024]{2,1,0:T(8,128)(2,1)}, u32[]{:S(2)}) copy-start(bf16[4,32,1024]{2,1,0:T(8,128)(2,1)} %param.16) | copy-start | bytes 786436
  7.2 33.8 %copy-start.2 = (bf16[4,32,1024]{2,1,0:T(8,128)(2,1)S(1)}, bf16[4,32,1024]{2,1,0:T(8,128)(2,1)}, u32[]{:S(2)}) copy-start(bf16[4,32,1024]{2,1,0:T(8,128)(2,1)} %param.13) | copy-start | bytes 786436
  7.2 673.8 %all-gather.2.cloned.1.call-start = ((), (), s32[]{:S(2)}) async-start(), calls=%async_computation.6 | async-start | bytes 6340608 | tf_op jit(solution)/shard_map/all_gather | solution.py:41
  10.2 24.4 %all-to-all-start = ((bf16[32,8,384]{2,1,0:T(8,128)(2,1)}), bf16[32,8,384]{2,1,0:T(8,128)(2,1)S(1)}, u32[]{:S(2)}, u32[]{:S(2)}) async-start(bf16[32,8,384]{2,1,0:T(8,128)(2,1)} %broadcast_in_dim.4), calls=%async_computation | async-start | bytes 393216 | tf_op jit(solution)/shard_map/all_to_all | solution.py:16
  35.6 17.1 %copy-start.6 = (bf16[128,16]{0,1:T(8,128)(2,1)S(1)}, bf16[128,16]{0,1:T(8,128)(2,1)}, u32[]{:S(2)}) copy-start(bf16[128,16]{0,1:T(8,128)(2,1)} %param.22) | copy-start | bytes 12292
  35.6 16.1 %all-to-all-start.1 = ((bf16[4,32,8,384]{3,2,1,0:T(8,128)(2,1)}), bf16[4,32,8,384]{3,2,1,0:T(8,128)(2,1)S(1)}, u32[]{:S(2)}, u32[]{:S(2)}) async-start(bf16[4,32,8,384]{3,2,1,0:T(8,128)(2,1)} %broadcast_in_dim.5), calls=%async_computation.1 | async-start | bytes 1572864 | tf_op jit(solution)/shard_map/all_to_all | solution.py:16
  41.0 13.2 %copy-start.3 = (bf16[4,32,1024]{2,1,0:T(8,128)(2,1)S(1)}, bf16[4,32,1024]{2,1,0:T(8,128)(2,1)}, u32[]{:S(2)}) copy-start(bf16[4,32,1024]{2,1,0:T(8,128)(2,1)} %broadcast_multiply_fusion) | copy-start | bytes 786436
  41.8 15.1 %copy-start.4 = (bf16[4,32,1024]{2,1,0:T(8,128)(2,1)S(1)}, bf16[4,32,1024]{2,1,0:T(8,128)(2,1)}, u32[]{:S(2)}) copy-start(bf16[4,32,1024]{2,1,0:T(8,128)(2,1)} %broadcast_multiply_fusion.1) | copy-start | bytes 786436
  41.8 639.3 %copy-start.7 = (bf16[128,16]{0,1:T(8,128)(2,1)S(1)}, bf16[128,16]{0,1:T(8,128)(2,1)}, u32[]{:S(2)}) copy-start(bf16[128,16]{0,1:T(8,128)(2,1)} %param.23) | copy-start | bytes 12292
  686.9 3.5 copy-start.5
  694.6 50.5 %all-to-all-start.2 = ((bf16[128,2,128]{2,1,0:T(2,128)(2,1)}), bf16[128,2,128]{2,1,0:T(2,128)(2,1)S(1)}, u32[]{:S(2)}, u32[]{:S(2)}) async-start(bf16[128,2,128]{2,1,0:T(2,128)(2,1)} %reshape.142), calls=%async_computation.2 | async-start | bytes 131072 | tf_op jit(solution)/shard_map/all_to_all | solution.py:178
  745.2 18.0 %all-to-all-start.3 = ((bf16[128,2,128]{2,1,0:T(2,128)(2,1)}), bf16[128,2,128]{2,1,0:T(2,128)(2,1)S(1)}, u32[]{:S(2)}, u32[]{:S(2)}) async-start(bf16[128,2,128]{2,1,0:T(2,128)(2,1)} %reshape.140), calls=%async_computation.3 | async-start | bytes 131072 | tf_op jit(solution)/shard_map/all_to_all | solution.py:179
  764.5 14.4 %all-to-all-start.4 = ((f32[4,32,4,512]{3,1,2,0:T(8,128)}), f32[4,32,4,512]{3,1,2,0:T(8,128)S(1)}, u32[]{:S(2)}, u32[]{:S(2)}) async-start(f32[4,32,4,512]{3,1,2,0:T(8,128)} %convolution_bitcast_fusion), calls=%async_computation.4 | async-start | bytes 2097152 | tf_op jit(solution)/shard_map/all_to_all | solution.py:55
  779.9 16.0 %all-to-all-start.5 = ((f32[32,4,512]{2,1,0:T(4,128)}), f32[32,4,512]{2,1,0:T(4,128)S(1)}, u32[]{:S(2)}, u32[]{:S(2)}) async-start(f32[32,4,512]{2,1,0:T(4,128)} %copy.46), calls=%async_computation.5 | async-start | bytes 524288 | tf_op jit(solution)/shard_map/all_to_all | solution.py:62
Sparse Core Ops, SparseCore 0:
  10.7 670.3 all-gather.1
where the time goes:
time: 804 us; the launch traced here: 803 us
  waiting for transfers between devices  687 us (85%)
  starting transfers between devices  71.2 us (9%)
  matrix products  18.6 us (2%)
  between operations  14.2 us (2%)
    all_gather x1, waiting for transfers between devices, side_by_side_2(): filled, at, done = (lax.all_gather(both, axis, axis=dim, tiled=True), 0, [])  623 us
    all_to_all x1, starting transfers between devices, body(): lax.all_to_all(train_normed, FSDP, split_axis=1, concat_axis=0, tiled=True)  38.9 us
    all_to_all x2, waiting for transfers between devices, sent_to_all(): return lax.all_to_all(copies, axis, split_axis=0, concat_axis=0, tiled=True)  20.6 us
    all_to_all x2, starting transfers between devices, sent_to_all(): return lax.all_to_all(copies, axis, split_axis=0, concat_axis=0, tiled=True)  17.6 us
  transfers between devices with their start and end apart: 7, of which 7 were waited for; matrix products, arithmetic and copies ran while one was open for 2% of the time, Pallas kernels for 0%

commit v1 on v0

v1 whole, which is shorter than its diff:
```python
import jax
import jax.numpy as jnp
from jax import lax
from jax.experimental import pallas as pl
from jax.experimental.pallas import tpu as pltpu
from jax.sharding import Mesh
from jax.sharding import PartitionSpec as P

AXES = ("y", "zl", "x", "zh", "core")
FSDP = ("y", "zl", "x")
DP_FSDP = ("zh", "core", "y", "zl", "x")
NY, NZ, NX = 8, 4, 4
SEQ = 32
EPS = 1e-06
BF, F32 = jnp.bfloat16, jnp.float32

ROWS = {"Y": (0, 32), "X": (32, 32), "Z": (64, 16)}
ORDER = {"Y": "xzy", "X": "yzx", "Z": "yxz"}
N_SEMS = 96
PARTNERS = 16

SCHEDULE = (
    [(q, s) for s in range(4) for q in "YXZ"]
    + [("X", 4), ("Z", 4), ("Y", 4), ("X", 5), ("Z", 5), ("X", 6), ("Z", 6), ("Y", 5), ("Y", 6)]
    + [("Z", 7), ("X", 7), ("Y", 7)]
    + [("Z", 8), ("X", 8), ("Y", 8)]
)


def nt(a, b):
    return lax.dot_general(a, b, (((1,), (1,)), ((), ())), preferred_element_type=F32)


def nn(a, b):
    return jnp.dot(a, b, preferred_element_type=F32)


def iota(shape, dim):
    return lax.broadcasted_iota(jnp.int32, shape, dim)


def one_hot_rows(rows, cols, per):
    return (iota((rows, cols), 0) // per == iota((rows, cols), 1)).astype(F32).astype(BF)


def kernel(
    xc, ct_c, len_c, xp, ct_p, len_p, down, up, win, wout, rk_down, rk_up,
    scores, feats,
    gath, xs, cot, masked, spread, taken, fblk, pblk, tsum, tgot, vsum, vgot,
    ld_sem, send_sem, recv_sem,
):
    y, zl, x = (lax.axis_index(a) for a in FSDP)
    zh, core = lax.axis_index("zh"), lax.axis_index("core")
    zz = zh * NZ + zl

    def at(dy=0, dx=0, dz=0, z_in=None, other=False):
        if z_in is None:
            full = lax.rem(zz + dz + 8, 8)
            tz, th = lax.rem(full, NZ), full // NZ
        else:
            tz, th = z_in, zh
        return (
            lax.rem(y + dy + NY, NY),
            tz,
            lax.rem(x + dx + NX, NX),
            th,
            1 - core if other else core,
        )

    loads = [
        pltpu.make_async_copy(src, dst, ld_sem.at[k])
        for k, (src, dst) in enumerate(
            (
                (ct_c, cot.at[pl.ds(0, 128)]),
                (ct_p, cot.at[pl.ds(128, 128)]),
                (xc, xs.at[pl.ds(0, 128)]),
                (xp, xs.at[pl.ds(128, 128)]),
            )
        )
    ]
    for c in loads:
        c.start()

    barrier = pltpu.get_barrier_semaphore()
    partners = [at(dy=d) for d in range(1, NY)] + [at(dx=d) for d in range(1, NX)]
    partners += [at(z_in=lax.rem(zl + d, NZ)) for d in range(1, NZ)]
    partners += [at(dz=1), at(dz=-1), at(other=True)]
    for dev in partners:
        pl.semaphore_signal(barrier, inc=1, device_id=dev, device_id_type=pl.DeviceIdType.MESH)

    ru = nt(one_hot_rows(16, 16, 1), rk_up[...])
    top, bottom = ru[0:8], ru[8:16]
    odd = lax.rem(x, 2) == 1
    left = jnp.where(odd, bottom, top)
    right = jnp.where(odd, top, bottom)
    dn = down[...]
    zero = jnp.zeros_like(dn)
    wide = jnp.concatenate(
        [jnp.concatenate([dn, zero], axis=1), jnp.concatenate([zero, dn], axis=1)], axis=0
    )
    fold = nt(jnp.concatenate([left, right], axis=1).astype(BF), wide)
    aux_1 = jnp.concatenate([fold, up[...].astype(F32)], axis=0)
    wo = wout[...].astype(F32)
    aux_0 = jnp.concatenate([wo[:, :128], wo[:, 128:]], axis=0)
    first = core == 0
    gath[core, y, zl, x, 0:64, :] = jnp.where(
        first, win[:, :128].astype(F32), win[:, 128:].astype(F32)
    ).astype(BF)
    gath[core, y, zl, x, 64:80, :] = jnp.where(first, aux_0, aux_1).astype(BF)

    pl.semaphore_wait(barrier, PARTNERS)

    used = [0]
    begun = []

    def send(src, dst, dev):
        k = used[0]
        used[0] += 1
        c = pltpu.make_async_remote_copy(
            src_ref=src,
            dst_ref=dst,
            send_sem=send_sem.at[k],
            recv_sem=recv_sem.at[k],
            device_id=dev,
            device_id_type=pl.DeviceIdType.MESH,
        )
        c.start()
        begun.append(c)
        return c

    size = {"x": NX, "y": NY, "z": NZ}
    here = {"x": x, "y": y, "z": zl}

    def block(q, phase, p, half):
        r0, n = ROWS[q]
        order = ORDER[q]
        idx = {}
        for a in order[:phase]:
            idx[a] = slice(None)
        for a in order[phase:]:
            idx[a] = here[a]
        idx[order[phase]] = p
        if half is not None:
            if phase == 0:
                if n >= 32:
                    r0, n = r0 + half * (n // 2), n // 2
                elif half == 1:
                    return None
            else:
                a = order[0]
                idx[a] = pl.ds(half * (size[a] // 2), size[a] // 2)
        return gath.at[core, idx["y"], idx["z"], idx["x"], pl.ds(r0, n), :]

    def steps(q):
        out = []
        for phase, a in enumerate(ORDER[q]):
            for t in range(1, size[a] // 2 + 1):
                out.append((phase, a, t))
        return out

    chain = {q: steps(q) for q in "YXZ"}
    flying = {q: [] for q in "YXZ"}
    swaps = []

    def swap(q, p):
        b = block(q, 2, p, None)
        swaps.append(send(b, b, at(other=True)))

    def advance(q, s):
        for c in flying[q]:
            c.wait_recv()
        flying[q] = []
        if s > 0:
            phase, a, t = chain[q][s - 1]
            if phase == 2:
                n = size[a]
                swap(q, lax.rem(here[a] - t + n, n))
                if t < n // 2:
                    swap(q, lax.rem(here[a] + t, n))
        if s < 8:
            phase, a, t = chain[q][s]
            n = size[a]
            if phase == 2 and t == 1:
                swap(q, here[a])
            last = t == n // 2
            for sign in (1, -1):
                p = lax.rem(here[a] - sign * (t - 1) + n, n)
                b = block(q, phase, p, (0 if sign == 1 else 1) if last else None)
                if b is not None:
                    flying[q].append(send(b, b, at(**{"d" + a: sign})))

    def mask_rows():
        loads[0].wait()
        loads[1].wait()
        pos = iota((SEQ, 1024), 0)
        for e in range(8):
            live = (len_c if e < 4 else len_p)[e % 4]
            rows = cot[e * SEQ : (e + 1) * SEQ, :].astype(F32)
            masked[e * SEQ : (e + 1) * SEQ, :] = jnp.where(pos < live, rows, 0.0).astype(BF)

    for k, (q, s) in enumerate(SCHEDULE):
        advance(q, s)
        if k == 2:
            mask_rows()
    loads[2].wait()
    loads[3].wait()
    for c in swaps:
        c.wait_recv()

    low = iota((8, 8, 128), 2) < 64

    def plane(k, acc):
        inward, right_sum, grad, outward = acc
        lanes = pl.ds(pl.multiple_of(k * 1024, 1024), 1024)
        xk = xs[:, lanes]
        w = jnp.concatenate(
            [gath[h, k, :, :, 0:64, :].reshape(1024, 128) for h in range(2)], axis=1
        )
        inward = inward + nn(xk, w)
        a0 = gath[0, k, :, :, 64:80, :].reshape(16, 16, 128).astype(F32)
        a1 = gath[1, k, :, :, 64:80, :].reshape(16, 16, 128).astype(F32)
        wo_k = jnp.concatenate(
            [a0[:, 0:8].reshape(128, 128), a0[:, 8:16].reshape(128, 128)], axis=1
        ).astype(BF)
        up_k = a1[:, 8:16].reshape(128, 128).astype(BF)
        pairs = a1[:, 0:8].reshape(8, 2, 8, 128)
        te, to = pairs[:, 0], pairs[:, 1]
        t8 = jnp.where(low, te, to)
        b8 = pltpu.roll(jnp.where(low, to, te), 64, 2)
        fold_t = jnp.concatenate(
            [jnp.concatenate([t8[m], b8[m]], axis=0) for m in range(8)], axis=1
        ).astype(BF)
        right_sum = right_sum + nt(xk, fold_t)
        mk = masked[:, pl.ds(pl.multiple_of(k * 128, 128), 128)]
        grad = grad + nn(mk, up_k)
        outward = outward + nn(mk, wo_k)
        return inward, right_sum, grad, outward

    zeros = lambda n: jnp.zeros((256, n), F32)
    inward, right_sum, grad, outward = lax.fori_loop(
        0, NY, plane, (zeros(256), zeros(16), zeros(128), zeros(256))
    )

    own = lax.rem(iota((128, 256), 0), 8) == iota((128, 256), 1) // SEQ
    spread_k = one_hot_rows(128, 16, 8)
    rd = nt(spread_k, rk_down[...]).astype(BF)
    left_t = jnp.where(own, nt(rd, grad.astype(BF)), 0.0).astype(BF)
    right_t = jnp.where(own, nt(spread_k, right_sum.astype(BF)), 0.0).astype(BF)
    gl = nn(left_t, inward.astype(BF))
    gr = nn(right_t, outward.astype(BF))
    joined = jnp.concatenate(
        [g[8 * k : 8 * k + 8] for g in (gl, gr) for k in range(16)], axis=1
    )
    inv = lax.rsqrt(jnp.sum(joined * joined, axis=1, keepdims=True) / 8192.0 + EPS)
    normed = joined * inv
    feats[...] = normed.astype(BF)

    for b in range(NY):
        part = normed[:, 1024 * b : 1024 * b + 1024]
        spread[b] = jnp.concatenate([part[:, :512], part[:, 512:]], axis=0).astype(BF)
    taken[y] = spread[y]
    moved = [
        send(spread.at[lax.rem(y + d, NY)], taken.at[y], at(dy=d)) for d in (4, 3, 5, 2, 6, 1, 7)
    ]
    for c in moved:
        c.wait_recv()
    upper = iota((8, 1024), 0) < 4
    f_rows, p_rows = [], []
    for m in range(4):
        a, b = (
            jnp.concatenate([v[0:8], v[8:16]], axis=1)
            for v in (taken[2 * m].astype(F32), taken[2 * m + 1].astype(F32))
        )
        f_rows.append(jnp.where(upper, a, pltpu.roll(b, 4, 0)))
        p_rows.append(jnp.where(upper, pltpu.roll(a, 4, 0), b))
    fblk[zl] = jnp.concatenate(f_rows, axis=0).astype(BF)
    pblk[x] = jnp.concatenate(p_rows, axis=0).astype(BF)
    moved = []
    for d in range(1, NZ):
        moved.append(send(fblk.at[zl], fblk.at[zl], at(z_in=lax.rem(zl + d, NZ))))
    for d in (2, 1, 3):
        moved.append(send(pblk.at[x], pblk.at[x], at(dx=d)))
    for c in moved:
        c.wait_recv()
    prod = nt(fblk[...].reshape(128, 1024), pblk[...].reshape(128, 1024))

    upper = iota((8, 128), 0) < 4
    tile = lambda zq, m: prod[zq * 32 + m * 8 : zq * 32 + m * 8 + 8]
    for m in range(4):
        for h in range(2):
            a, b = tile(2 * h, m), tile(2 * h + 1, m)
            tsum[2 * m, 8 * h : 8 * h + 8] = jnp.where(upper, a, pltpu.roll(b, 4, 0))
            tsum[2 * m + 1, 8 * h : 8 * h + 8] = jnp.where(upper, pltpu.roll(a, 4, 0), b)
    tgot[y] = tsum[y]
    moved = [
        send(tsum.at[lax.rem(y + d, NY)], tgot.at[y], at(dy=d)) for d in (4, 3, 5, 2, 6, 1, 7)
    ]
    for c in moved:
        c.wait_recv()
    total = tgot[0]
    for k in range(1, NY):
        total = total + tgot[k]
    vsum[0] = total[0:8]
    vsum[1] = total[8:16]
    vgot[zl] = vsum[zl // 2]
    moved = []
    for d in range(1, NZ):
        tz = lax.rem(zl + d, NZ)
        moved.append(send(vsum.at[tz // 2], vgot.at[zl], at(z_in=tz)))

    src, col = iota((512, 512), 0), iota((512, 512), 1)
    want = ((col // 16) % 4) * 128 + ((col // 4) % 4) * 32 + (col // 64) * 4 + col % 4
    perm = (src == want).astype(F32).astype(BF)
    for c in moved:
        c.wait_recv()
    odd_z = lax.rem(zl, 2) == 1
    flat = jnp.concatenate(
        [jnp.where(odd_z, pltpu.roll(vgot[k], 4, 0), vgot[k]) for k in range(NZ)], axis=1
    )
    p1 = flat.astype(BF)
    rest = flat - p1.astype(F32)
    p2 = rest.astype(BF)
    p3 = (rest - p2.astype(F32)).astype(BF)
    out = nn(p1, perm) + nn(p2, perm) + nn(p3, perm)
    scores[...] = out * (1.0 / 8192.0)

    for c in begun:
        c.wait_send()


def body(xc, ct_c, len_c, xp, ct_p, len_p, down, up, win, wout, rk_down, rk_up):
    width, values = xc.shape[2], ct_c.shape[2]
    anyspace = pl.BlockSpec(memory_space=pl.ANY)
    vmem = pl.BlockSpec(memory_space=pltpu.VMEM)
    smem = pl.BlockSpec(memory_space=pltpu.SMEM)
    scores, feats = pl.pallas_call(
        kernel,
        out_shape=(
            jax.ShapeDtypeStruct((8, 512), F32),
            jax.ShapeDtypeStruct((8, 8192), BF),
        ),
        in_specs=[anyspace, anyspace, smem, anyspace, anyspace, smem] + [vmem] * 6,
        out_specs=(vmem, vmem),
        scratch_shapes=[
            pltpu.VMEM((2, NY, NZ, NX, 80, 128), BF),
            pltpu.VMEM((256, 8192), BF),
            pltpu.VMEM((256, 1024), BF),
            pltpu.VMEM((256, 1024), BF),
            pltpu.VMEM((NY, 16, 512), BF),
            pltpu.VMEM((NY, 16, 512), BF),
            pltpu.VMEM((NZ, 32, 1024), BF),
            pltpu.VMEM((NX, 32, 1024), BF),
            pltpu.VMEM((NY, 16, 128), F32),
            pltpu.VMEM((NY, 16, 128), F32),
            pltpu.VMEM((2, 8, 128), F32),
            pltpu.VMEM((NZ, 8, 128), F32),
            pltpu.SemaphoreType.DMA((4,)),
            pltpu.SemaphoreType.DMA((N_SEMS,)),
            pltpu.SemaphoreType.DMA((N_SEMS,)),
        ],
        compiler_params=pltpu.CompilerParams(
            collective_id=0, has_side_effects=True, vmem_limit_bytes=48 * 1024 * 1024
        ),
        name="lora_scores",
    )(
        xc.reshape(-1, width), ct_c.reshape(-1, values), len_c,
        xp.reshape(-1, width), ct_p.reshape(-1, values), len_p,
        down, up, win, wout, rk_down, rk_up,
    )
    return scores[:4], feats[:4]


def solution(mesh):
    split = Mesh(mesh.devices.reshape(NY, NZ, NX, 2, 2), AXES)
    rows = P(FSDP, None)
    whole = P(DP_FSDP, None, None)
    return jax.shard_map(
        body,
        mesh=split,
        in_specs=(
            whole, whole, P(DP_FSDP), whole, whole, P(DP_FSDP), rows, rows, rows, rows, P(), P(),
        ),
        out_specs=(P(DP_FSDP, None), P(DP_FSDP, None)),
        check_vma=False,
    )
```

time: 804 us -> 90.7 us (0.11)
  waiting for transfers between devices: 687 us -> 0 us
  Pallas kernels: 0 us -> 77.4 us
  starting transfers between devices: 71.2 us -> 0 us
  matrix products: 18.6 us -> 0 us
  between operations: 14.2 us -> 0.65 us
    all_gather x1 -> x0, waiting for transfers between devices: 623 us -> none  [side_by_side_2(): filled, at, done = (lax.all_gather(both, axis, axis=dim, tiled=True), 0, [])]
    pallas_call x0 -> x1, Pallas kernels: none -> 77.4 us  [body(): pl.pallas_call(kernel, out_shape=(jax.ShapeDtypeStruct((8, 512), F32), ja...]
    all_to_all x6 -> x0, starting transfers between devices: 71.1 us -> none  [the longest x1 38.9 us: body(): lax.all_to_all(train_normed, FSDP, split_axis=1, concat_axis=0, tiled=True)]
    all_to_all x6 -> x0, waiting for transfers between devices: 63.9 us -> none  [the longest x2 20.6 us: sent_to_all(): return lax.all_to_all(copies, axis, split_axis=0, concat_axis=0, tiled=True)]
    dot_general x13 -> x0, matrix products: 18.6 us -> none  [the longest x2 5.55 us: compute_sketch_features(): jnp.dot(down_round, rank_sketch_up, preferred_element_type=jnp.float32)]
    unnamed x23 -> x22, local copies, waits for them, and re-layouts: 1.81 us -> 10.8 us
  transfers between devices with their start and end apart: 7 -> 0, of which waited for: 7 -> 0; matrix products, arithmetic and copies ran while one was open for 2% -> 0% of each run, Pallas kernels for 0% -> 0%
where the time goes in v1:
time: 90.7 us; the launch traced here: 90.2 us
  Pallas kernels  77.4 us (85%)
  local copies, waits for them, and re-layouts  12.1 us (13%)
    pallas_call x1, Pallas kernels, body(): pl.pallas_call(kernel, out_shape=(jax.ShapeDtypeStruct((8, 512), F32), ja...  77.4 us
    unnamed x22, local copies, waits for them, and re-layouts  10.8 us

profile of v1, /device:TPU:8, one launch (start us, length us, event | category | flops | bytes accessed | tf_op | source)
XLA Modules:
  0.0 90.2 jit_solution(5995507762180476500)
XLA Ops:
  0.6 0.8 copy.14.rk_down
  1.4 0.8 copy.15.rk_up
  2.2 0.0 copy-start
  2.2 1.6 %copy-done = bf16[4,32,8192]{2,1,0:T(8,128)(2,1)S(1)} copy-done((bf16[4,32,8192]{2,1,0:T(8,128)(2,1)S(1)}, bf16[4,32,8192]{2,1,0:T(8,128)(2,1)}, u32[]{:S(2)}) %copy-start) | copy-done | bytes 2097176
  3.8 0.0 copy-start.1
  3.8 1.6 %copy-done.1 = bf16[4,32,8192]{2,1,0:T(8,128)(2,1)S(1)} copy-done((bf16[4,32,8192]{2,1,0:T(8,128)(2,1)S(1)}, bf16[4,32,8192]{2,1,0:T(8,128)(2,1)}, u32[]{:S(2)}) %copy-start.1) | copy-done | bytes 2097176
  5.4 0.0 copy-start.2
  5.4 0.9 %copy-done.2 = bf16[4,32,1024]{2,1,0:T(8,128)(2,1)S(1)} copy-done((bf16[4,32,1024]{2,1,0:T(8,128)(2,1)S(1)}, bf16[4,32,1024]{2,1,0:T(8,128)(2,1)}, u32[]{:S(2)}) %copy-start.2) | copy-done | bytes 262168
  6.4 0.0 copy-start.3
  6.4 0.9 %copy-done.3 = bf16[4,32,1024]{2,1,0:T(8,128)(2,1)S(1)} copy-done((bf16[4,32,1024]{2,1,0:T(8,128)(2,1)S(1)}, bf16[4,32,1024]{2,1,0:T(8,128)(2,1)}, u32[]{:S(2)}) %copy-start.3) | copy-done | bytes 262168
  7.3 0.0 copy-start.4
  7.3 0.8 copy-done.4
  8.1 0.0 copy-start.5
  8.1 0.7 copy-done.5
  8.8 0.0 copy-start.6
  8.8 0.7 copy-done.6
  9.5 0.0 copy-start.7
  9.5 0.7 copy-done.7
  10.2 0.0 copy-start.8
  10.2 0.7 copy-done.8
  10.8 0.0 copy-start.9
  10.8 0.7 copy-done.9
  11.5 77.4 %lora_scores.1 = (f32[8,512]{1,0:T(8,128)S(1)}, bf16[8,8192]{1,0:T(8,128)(2,1)S(1)}) custom-call(bf16[128,8192]{1,0:T(8,128)(2,1)S(1)} %bitcast.4, bf16[128,1024]{1,0:T(8,128)(2,1)S(1)} %bitcast.6, s32[4]{0:T(128)S(1)} %copy-done.8, bf16[128,8192]{1,0:T(8,128)(2,1)S(1)} %bitcast.5, bf16[128,1024]{1,0:T(8,128)(2,1)S(1)} %bitcast.7, s32[4]{0:T(128)S(1)} %copy-done.9, ...), custom_call_target="tpu_custom_call" | custom-call | tf_op jit(solution)/shard_map/lora_scores/pallas_call | solution.py:336
  88.9 0.6 slice.6
  89.5 0.6 slice.7
Async XLA Ops:
  2.2 1.6 %copy-start = (bf16[4,32,8192]{2,1,0:T(8,128)(2,1)S(1)}, bf16[4,32,8192]{2,1,0:T(8,128)(2,1)}, u32[]{:S(2)}) copy-start(bf16[4,32,8192]{2,1,0:T(8,128)(2,1)} %param.12) | copy-start | bytes 6291460
  3.8 1.6 %copy-start.1 = (bf16[4,32,8192]{2,1,0:T(8,128)(2,1)S(1)}, bf16[4,32,8192]{2,1,0:T(8,128)(2,1)}, u32[]{:S(2)}) copy-start(bf16[4,32,8192]{2,1,0:T(8,128)(2,1)} %param.15) | copy-start | bytes 6291460
  5.4 0.9 %copy-start.2 = (bf16[4,32,1024]{2,1,0:T(8,128)(2,1)S(1)}, bf16[4,32,1024]{2,1,0:T(8,128)(2,1)}, u32[]{:S(2)}) copy-start(bf16[4,32,1024]{2,1,0:T(8,128)(2,1)} %param.13) | copy-start | bytes 786436
  6.4 0.9 %copy-start.3 = (bf16[4,32,1024]{2,1,0:T(8,128)(2,1)S(1)}, bf16[4,32,1024]{2,1,0:T(8,128)(2,1)}, u32[]{:S(2)}) copy-start(bf16[4,32,1024]{2,1,0:T(8,128)(2,1)} %param.16) | copy-start | bytes 786436
  7.3 0.8 copy-start.4
  8.1 0.7 copy-start.5
  8.8 0.7 copy-start.6
  9.5 0.7 copy-start.7
  10.2 0.7 copy-start.8
  10.8 0.7 copy-start.9

commit v2 on v1

--- a/solution.py
+++ b/solution.py
@@ -14,17 +14,7 @@
 EPS = 1e-06
 BF, F32 = jnp.bfloat16, jnp.float32
 
-ROWS = {"Y": (0, 32), "X": (32, 32), "Z": (64, 16)}
-ORDER = {"Y": "xzy", "X": "yzx", "Z": "yxz"}
-N_SEMS = 96
-PARTNERS = 16
-
-SCHEDULE = (
-    [(q, s) for s in range(4) for q in "YXZ"]
-    + [("X", 4), ("Z", 4), ("Y", 4), ("X", 5), ("Z", 5), ("X", 6), ("Z", 6), ("Y", 5), ("Y", 6)]
-    + [("Z", 7), ("X", 7), ("Y", 7)]
-    + [("Z", 8), ("X", 8), ("Y", 8)]
-)
+N_SEMS = 192
 
 
 def nt(a, b):
@@ -44,8 +34,9 @@
 
 
 def kernel(
-    xc, ct_c, len_c, xp, ct_p, len_p, down, up, win, wout, rk_down, rk_up,
+    xc, ct_c, len_ch, xp, ct_p, len_ph, down_h, up_h, win_h, wout_h, rk_down_h, rk_up_h,
     scores, feats,
+    len_c, len_p, down, up, wout, rk_down, rk_up,
     gath, xs, cot, masked, spread, taken, fblk, pblk, tsum, tgot, vsum, vgot,
     ld_sem, send_sem, recv_sem,
 ):
@@ -71,6 +62,14 @@
         pltpu.make_async_copy(src, dst, ld_sem.at[k])
         for k, (src, dst) in enumerate(
             (
+                (rk_up_h, rk_up),
+                (down_h, down),
+                (up_h, up),
+                (win_h.at[:, pl.ds(pl.multiple_of(core * 128, 128), 128)], gath.at[core, y, zl, x, pl.ds(0, 64)]),
+                (wout_h, wout),
+                (rk_down_h, rk_down),
+                (len_ch, len_c),
+                (len_ph, len_p),
                 (ct_c, cot.at[pl.ds(0, 128)]),
                 (ct_p, cot.at[pl.ds(128, 128)]),
                 (xc, xs.at[pl.ds(0, 128)]),
@@ -84,11 +83,14 @@
     barrier = pltpu.get_barrier_semaphore()
     partners = [at(dy=d) for d in range(1, NY)] + [at(dx=d) for d in range(1, NX)]
     partners += [at(z_in=lax.rem(zl + d, NZ)) for d in range(1, NZ)]
-    partners += [at(dz=1), at(dz=-1), at(other=True)]
+    partners += [at(dz=d) for d in (1, -1, 2, -2)] + [at(other=True)]
     for dev in partners:
         pl.semaphore_signal(barrier, inc=1, device_id=dev, device_id_type=pl.DeviceIdType.MESH)
 
-    ru = nt(one_hot_rows(16, 16, 1), rk_up[...])
+    for c in loads[:8]:
+        c.wait()
+
+    ru = rk_up[...].astype(F32)
     top, bottom = ru[0:8], ru[8:16]
     odd = lax.rem(x, 2) == 1
     left = jnp.where(odd, bottom, top)
@@ -103,12 +105,9 @@
     wo = wout[...].astype(F32)
     aux_0 = jnp.concatenate([wo[:, :128], wo[:, 128:]], axis=0)
     first = core == 0
-    gath[core, y, zl, x, 0:64, :] = jnp.where(
-        first, win[:, :128].astype(F32), win[:, 128:].astype(F32)
-    ).astype(BF)
     gath[core, y, zl, x, 64:80, :] = jnp.where(first, aux_0, aux_1).astype(BF)
 
-    pl.semaphore_wait(barrier, PARTNERS)
+    pl.semaphore_wait(barrier, len(partners))
 
     used = [0]
     begun = []
@@ -128,82 +127,149 @@
         begun.append(c)
         return c
 
-    size = {"x": NX, "y": NY, "z": NZ}
-    here = {"x": x, "y": y, "z": zl}
-
-    def block(q, phase, p, half):
-        r0, n = ROWS[q]
-        order = ORDER[q]
-        idx = {}
-        for a in order[:phase]:
-            idx[a] = slice(None)
-        for a in order[phase:]:
-            idx[a] = here[a]
-        idx[order[phase]] = p
-        if half is not None:
-            if phase == 0:
-                if n >= 32:
-                    r0, n = r0 + half * (n // 2), n // 2
-                elif half == 1:
-                    return None
-            else:
-                a = order[0]
-                idx[a] = pl.ds(half * (size[a] // 2), size[a] // 2)
-        return gath.at[core, idx["y"], idx["z"], idx["x"], pl.ds(r0, n), :]
-
-    def steps(q):
-        out = []
-        for phase, a in enumerate(ORDER[q]):
-            for t in range(1, size[a] // 2 + 1):
-                out.append((phase, a, t))
-        return out
-
-    chain = {q: steps(q) for q in "YXZ"}
-    flying = {q: [] for q in "YXZ"}
-    swaps = []
-
-    def swap(q, p):
-        b = block(q, 2, p, None)
-        swaps.append(send(b, b, at(other=True)))
-
-    def advance(q, s):
-        for c in flying[q]:
-            c.wait_recv()
-        flying[q] = []
-        if s > 0:
-            phase, a, t = chain[q][s - 1]
-            if phase == 2:
-                n = size[a]
-                swap(q, lax.rem(here[a] - t + n, n))
-                if t < n // 2:
-                    swap(q, lax.rem(here[a] + t, n))
-        if s < 8:
-            phase, a, t = chain[q][s]
-            n = size[a]
-            if phase == 2 and t == 1:
-                swap(q, here[a])
-            last = t == n // 2
-            for sign in (1, -1):
-                p = lax.rem(here[a] - sign * (t - 1) + n, n)
-                b = block(q, phase, p, (0 if sign == 1 else 1) if last else None)
-                if b is not None:
-                    flying[q].append(send(b, b, at(**{"d" + a: sign})))
-
     def mask_rows():
-        loads[0].wait()
-        loads[1].wait()
+        loads[8].wait()
+        loads[9].wait()
         pos = iota((SEQ, 1024), 0)
         for e in range(8):
             live = (len_c if e < 4 else len_p)[e % 4]
             rows = cot[e * SEQ : (e + 1) * SEQ, :].astype(F32)
             masked[e * SEQ : (e + 1) * SEQ, :] = jnp.where(pos < live, rows, 0.0).astype(BF)
 
-    for k, (q, s) in enumerate(SCHEDULE):
-        advance(q, s)
-        if k == 2:
-            mask_rows()
-    loads[2].wait()
-    loads[3].wait()
+    every = slice(None)
+    ring = lambda p, n: lax.rem(p + n, n)
+
+    def rows_a(p, zq, xs=every):
+        return gath.at[core, p, zq, xs, pl.ds(0, 32)]
+
+    def rows_b(lo, n, zq, xq):
+        return gath.at[core, pl.ds(lo, n), zq, xq, pl.ds(32, 48)]
+
+    swaps = []
+
+    def swap(ref):
+        swaps.append(send(ref, ref, at(other=True)))
+
+    def out(ref, **d):
+        return send(ref, ref, at(**d))
+
+    def arrived(*copies):
+        for c in copies:
+            c.wait_recv()
+
+    def a_plane(zq):
+        ref = rows_a(y, zq)
+        swap(ref)
+        return zq, {d: out(ref, dy=d) for d in (2, -2, 1, -1)}
+
+    def a_forward(chunk):
+        zq, flying = chunk
+        on = {}
+        for sign, xs in ((1, pl.ds(0, 2)), (-1, pl.ds(2, 2))):
+            p = ring(y - 2 * sign, NY)
+            arrived(flying[2 * sign])
+            on[sign] = (out(rows_a(p, zq, xs), dy=2 * sign), out(rows_a(p, zq), dy=sign))
+            swap(rows_a(p, zq))
+        return zq, on
+
+    def a_near(chunk):
+        zq, flying = chunk
+        for sign in (1, -1):
+            arrived(flying[sign])
+            swap(rows_a(ring(y - sign, NY), zq))
+
+    def a_far(chunk):
+        zq, on = chunk
+        for sign in (1, -1):
+            arrived(on[sign][1])
+            swap(rows_a(ring(y - 3 * sign, NY), zq))
+        arrived(on[1][0], on[-1][0])
+        swap(rows_a(ring(y + 4, NY), zq))
+
+    def over_z(lo, zq, xq):
+        ref = rows_b(lo, 4, zq, xq)
+        return (
+            out(ref, dz=1),
+            out(ref, dz=-1),
+            out(rows_b(lo, 2, zq, xq), dz=2),
+            out(rows_b(lo + 2, 2, zq, xq), dz=-2),
+        )
+
+    def over_x(lo, zq, xq):
+        ref = rows_b(lo, 4, zq, xq)
+        return tuple(out(ref, dx=d) for d in (2, 1, 3))
+
+    z_from = (ring(zl - 1, NZ), ring(zl + 1, NZ), ring(zl + 2, NZ))
+    x_from = (ring(x - 2, NX), ring(x - 1, NX), ring(x - 3, NX))
+
+    own_a = rows_a(y, zl, x)
+    own_b = gath.at[core, y, zl, x, pl.ds(32, 48)]
+    a1 = [out(own_a, dx=d) for d in (2, 1, 3)]
+    b1 = [out(own_b, dy=d) for d in (4, 3, 5, 2, 6, 1, 7)]
+    mask_rows()
+    arrived(*a1)
+    mine = rows_a(y, zl)
+    a2 = (
+        out(mine, dz=1),
+        out(mine, dz=-1),
+        out(rows_a(y, zl, pl.ds(0, 2)), dz=2),
+        out(rows_a(y, zl, pl.ds(2, 2)), dz=-2),
+    )
+    chunk0 = a_plane(zl)
+    arrived(*b1)
+    bx2 = over_z(0, zl, x)
+    bz2 = over_x(4, zl, x)
+    bx3 = [(zl, over_x(0, zl, x))]
+    bz3 = [(x, over_z(4, zl, x))]
+    swap(rows_b(0, 8, zl, x))
+    arrived(a2[0])
+    chunk1 = a_plane(z_from[0])
+    arrived(a2[1])
+    chunk2 = a_plane(z_from[1])
+    arrived(a2[2], a2[3])
+    chunk3 = a_plane(z_from[2])
+    far = [a_forward(chunk0)]
+    a_near(chunk0)
+
+    def bx_next(zq):
+        bx3.append((zq, over_x(0, zq, x)))
+        swap(rows_b(0, 4, zq, x))
+
+    def bz_next(xq):
+        bz3.append((xq, over_z(4, zl, xq)))
+        swap(rows_b(4, 4, zl, xq))
+
+    for k in range(2):
+        arrived(bx2[k])
+        bx_next(z_from[k])
+        arrived(bz2[1 + k])
+        bz_next(x_from[1 + k])
+    arrived(bz2[0])
+    bz_next(x_from[0])
+    arrived(bx2[2], bx2[3])
+    bx_next(z_from[2])
+    for chunk in (chunk1, chunk2, chunk3):
+        far.append(a_forward(chunk))
+        a_near(chunk)
+
+    def b_last(k):
+        zq, flying = bx3[k]
+        for c, xq in zip(flying, x_from):
+            arrived(c)
+            swap(rows_b(0, 4, zq, xq))
+        xq, flying = bz3[k]
+        arrived(flying[0])
+        swap(rows_b(4, 4, z_from[0], xq))
+        arrived(flying[1])
+        swap(rows_b(4, 4, z_from[1], xq))
+        arrived(flying[2], flying[3])
+        swap(rows_b(4, 4, z_from[2], xq))
+
+    for k in range(4):
+        b_last(k)
+        a_far(far[k])
+    loads[10].wait()
+    loads[11].wait()
     for c in swaps:
         c.wait_recv()
 
@@ -243,7 +309,7 @@
 
     own = lax.rem(iota((128, 256), 0), 8) == iota((128, 256), 1) // SEQ
     spread_k = one_hot_rows(128, 16, 8)
-    rd = nt(spread_k, rk_down[...]).astype(BF)
+    rd = nn(spread_k, rk_down[...]).astype(BF)
     left_t = jnp.where(own, nt(rd, grad.astype(BF)), 0.0).astype(BF)
     right_t = jnp.where(own, nt(spread_k, right_sum.astype(BF)), 0.0).astype(BF)
     gl = nn(left_t, inward.astype(BF))
@@ -332,16 +398,22 @@
     width, values = xc.shape[2], ct_c.shape[2]
     anyspace = pl.BlockSpec(memory_space=pl.ANY)
     vmem = pl.BlockSpec(memory_space=pltpu.VMEM)
-    smem = pl.BlockSpec(memory_space=pltpu.SMEM)
     scores, feats = pl.pallas_call(
         kernel,
         out_shape=(
             jax.ShapeDtypeStruct((8, 512), F32),
             jax.ShapeDtypeStruct((8, 8192), BF),
         ),
-        in_specs=[anyspace, anyspace, smem, anyspace, anyspace, smem] + [vmem] * 6,
+        in_specs=[anyspace] * 12,
         out_specs=(vmem, vmem),
         scratch_shapes=[
+            pltpu.SMEM((4,), jnp.int32),
+            pltpu.SMEM((4,), jnp.int32),
+            pltpu.VMEM((64, 128), BF),
+            pltpu.VMEM((8, 128), BF),
+            pltpu.VMEM((8, 256), BF),
+            pltpu.VMEM((16, 128), BF),
+            pltpu.VMEM((16, 128), BF),
             pltpu.VMEM((2, NY, NZ, NX, 80, 128), BF),
             pltpu.VMEM((256, 8192), BF),
             pltpu.VMEM((256, 1024), BF),
@@ -354,18 +426,18 @@
             pltpu.VMEM((NY, 16, 128), F32),
             pltpu.VMEM((2, 8, 128), F32),
             pltpu.VMEM((NZ, 8, 128), F32),
-            pltpu.SemaphoreType.DMA((4,)),
+            pltpu.SemaphoreType.DMA((12,)),
             pltpu.SemaphoreType.DMA((N_SEMS,)),
             pltpu.SemaphoreType.DMA((N_SEMS,)),
         ],
         compiler_params=pltpu.CompilerParams(
-            collective_id=0, has_side_effects=True, vmem_limit_bytes=48 * 1024 * 1024
+            collective_id=0, has_side_effects=True, vmem_limit_bytes=67043328
         ),
         name="lora_scores",
     )(
         xc.reshape(-1, width), ct_c.reshape(-1, values), len_c,
         xp.reshape(-1, width), ct_p.reshape(-1, values), len_p,
-        down, up, win, wout, rk_down, rk_up,
+        down, up, win, wout, rk_down.T, rk_up.T,
     )
     return scores[:4], feats[:4]
 

time: 90.7 us -> 69.4 us (0.77)
  Pallas kernels: 77.4 us -> 65.7 us
  local copies, waits for them, and re-layouts: 12.1 us -> 2.87 us
    pallas_call x1, Pallas kernels: 77.4 us -> 65.7 us  [body(): pl.pallas_call(kernel, out_shape=(jax.ShapeDtypeStruct((8, 512), F32), ja...]
    unnamed x22 -> x0, local copies, waits for them, and re-layouts: 10.8 us -> none
    slice x2, local copies, waits for them, and re-layouts: 1.25 us -> 2.87 us  [body(): return (scores[:4], feats[:4])]
where the time goes in v2:
time: 69.4 us; the launch traced here: 69.2 us
  Pallas kernels  65.7 us (95%)
  local copies, waits for them, and re-layouts  2.87 us (4%)
    pallas_call x1, Pallas kernels, body(): pl.pallas_call(kernel, out_shape=(jax.ShapeDtypeStruct((8, 512), F32), ja...  65.7 us
    slice x2, local copies, waits for them, and re-layouts, body(): return (scores[:4], feats[:4])  2.87 us

profile of v2, /device:TPU:8, one launch (start us, length us, event | category | flops | bytes accessed | tf_op | source)
XLA Modules:
  0.0 69.2 jit_solution(12146013653340674995)
XLA Ops:
  0.6 65.7 %lora_scores.1 = (f32[8,512]{1,0:T(8,128)}, bf16[8,8192]{1,0:T(8,128)(2,1)}) custom-call(bf16[128,8192]{1,0:T(8,128)(2,1)} %bitcast.6, bf16[128,1024]{1,0:T(8,128)(2,1)} %bitcast.8, s32[4]{0:T(128)} %len_ch.1, bf16[128,8192]{1,0:T(8,128)(2,1)} %bitcast.7, bf16[128,1024]{1,0:T(8,128)(2,1)} %bitcast.9, s32[4]{0:T(128)} %len_ph.1, bf16[64,128]{1,0:T(8,128)(2,1)} %down_h.1, ...), custom_call_target="tpu_custom_call" | custom-call | tf_op jit(solution)/shard_map/lora_scores/pallas_call | solution.py:401
  66.3 1.3 %slice.6 = f32[4,512]{1,0:T(4,128)} slice(f32[8,512]{1,0:T(8,128)} %get-tuple-element.4), slice={[0:4], [0:512]} | slice | bytes 16384 | tf_op jit(solution)/shard_map/slice | solution.py:442
  67.6 1.6 %slice.7 = bf16[4,8192]{1,0:T(4,128)(2,1)} slice(bf16[8,8192]{1,0:T(8,128)(2,1)} %get-tuple-element.5), slice={[0:4], [0:8192]} | slice | bytes 131072 | tf_op jit(solution)/shard_map/slice | solution.py:442

commit v3 on v2

v3 whole, which is shorter than its diff:
```python
import jax
import jax.numpy as jnp
from jax import lax
from jax.experimental import pallas as pl
from jax.experimental.pallas import tpu as pltpu
from jax.sharding import Mesh
from jax.sharding import PartitionSpec as P

AXES = ("y", "zl", "x", "zh", "core")
FSDP = ("y", "zl", "x")
DP_FSDP = ("zh", "core", "y", "zl", "x")
NY, NZ, NX = 8, 4, 4
SEQ = 32
EPS = 1e-06
BF, F32 = jnp.bfloat16, jnp.float32

N_SEND, N_RECV = 13, 47


def nt(a, b):
    return lax.dot_general(a, b, (((1,), (1,)), ((), ())), preferred_element_type=F32)


def nn(a, b):
    return jnp.dot(a, b, preferred_element_type=F32)


def iota(shape, dim):
    return lax.broadcasted_iota(jnp.int32, shape, dim)


def one_hot_rows(rows, cols, per):
    return (iota((rows, cols), 0) // per == iota((rows, cols), 1)).astype(F32).astype(BF)


def kernel(
    xc, ct_c, len_ch, xp, ct_p, len_ph, down_h, up_h, win_h, wout_h, rk_down_h, rk_up_h,
    scores, feats,
    len_c, len_p, down, up, wout, rk_down, rk_up,
    gath, xs, cot, masked, f_out, p_out, fblk, pblk, tsum, tgot, vsum, vgot, perm,
    ld_sem, send_sem, recv_sem,
):
    y, zl, x = (lax.axis_index(a) for a in FSDP)
    zh, core = lax.axis_index("zh"), lax.axis_index("core")
    zz = zh * NZ + zl

    def at(dy=0, dx=0, dz=0, z_in=None, other=False):
        if z_in is None:
            full = lax.rem(zz + dz + 8, 8)
            tz, th = lax.rem(full, NZ), full // NZ
        else:
            tz, th = z_in, zh
        return (
            lax.rem(y + dy + NY, NY),
            tz,
            lax.rem(x + dx + NX, NX),
            th,
            1 - core if other else core,
        )

    loads = [
        pltpu.make_async_copy(src, dst, ld_sem.at[k])
        for k, (src, dst) in enumerate(
            (
                (win_h.at[:, pl.ds(pl.multiple_of(core * 128, 128), 128)], gath.at[core, y, zl, x, pl.ds(0, 64)]),
                (rk_up_h, rk_up),
                (down_h, down),
                (up_h, up),
                (wout_h, wout),
                (rk_down_h, rk_down),
                (len_ch, len_c),
                (len_ph, len_p),
                (ct_c, cot.at[pl.ds(0, 128)]),
                (ct_p, cot.at[pl.ds(128, 128)]),
                (xc, xs.at[pl.ds(0, 128)]),
                (xp, xs.at[pl.ds(128, 128)]),
            )
        )
    ]
    for c in loads:
        c.start()

    barrier = pltpu.get_barrier_semaphore()
    partners = [at(dy=d) for d in range(1, NY)] + [at(dx=d) for d in range(1, NX)]
    partners += [at(z_in=lax.rem(zl + d, NZ)) for d in range(1, NZ)]
    partners += [at(dz=d) for d in (1, -1, 2, -2)] + [at(other=True)]
    for dev in partners:
        pl.semaphore_signal(barrier, inc=1, device_id=dev, device_id_type=pl.DeviceIdType.MESH)

    loads[0].wait()
    pl.semaphore_wait(barrier, len(partners))

    names = {}

    def key(kind, name):
        return names.setdefault(kind, {}).setdefault(name, len(names.get(kind, {})))

    def send(src, dst, dev, group, arrival):
        pltpu.make_async_remote_copy(
            src_ref=src,
            dst_ref=dst,
            send_sem=send_sem.at[key("send", group)],
            recv_sem=recv_sem.at[key("recv", arrival)],
            device_id=dev,
            device_id_type=pl.DeviceIdType.MESH,
        ).start()

    def arrived(arrival, ref):
        pltpu.make_async_copy(ref, ref, recv_sem.at[key("recv", arrival)]).wait()

    def left(group, ref):
        pltpu.make_async_copy(ref, ref, send_sem.at[key("send", group)]).wait()

    def mask_rows():
        loads[8].wait()
        loads[9].wait()
        pos = iota((SEQ, 1024), 0)
        for e in range(8):
            live = (len_c if e < 4 else len_p)[e % 4]
            rows = cot[e * SEQ : (e + 1) * SEQ, :].astype(F32)
            masked[e * SEQ : (e + 1) * SEQ, :] = jnp.where(pos < live, rows, 0.0).astype(BF)

    every = slice(None)
    ring = lambda p, n: lax.rem(p + n, n)

    def rows_a(p, zq, xs=every):
        return gath.at[core, p, zq, xs, pl.ds(0, 32)]

    def rows_b(lo, n, zq, xq):
        return gath.at[core, pl.ds(lo, n), zq, xq, pl.ds(32, 48)]

    def swap(ref):
        send(ref, ref, at(other=True), "swap", "swap")

    def out(ref, group, arrival, **d):
        send(ref, ref, at(**d), group, arrival)

    def a_plane(zq, c):
        ref = rows_a(y, zq)
        swap(ref)
        for d in (2, -2):
            out(ref, "plane", ("two", c, d), dy=d)
        for d in (1, -1):
            out(ref, "plane", ("near", c), dy=d)

    def a_forward(zq, c):
        for sign, lo in ((1, 0), (-1, 2)):
            ref = rows_a(ring(y - 2 * sign, NY), zq)
            arrived(("two", c, 2 * sign), ref)
            out(rows_a(ring(y - 2 * sign, NY), zq, pl.ds(lo, 2)), "forward", ("far", c), dy=2 * sign)
            out(ref, "forward", ("far", c), dy=sign)
            swap(ref)

    def a_near(zq, c):
        arrived(("near", c), gath.at[core, pl.ds(0, 2), zq, :, pl.ds(0, 32)])
        for d in (1, -1):
            swap(rows_a(ring(y + d, NY), zq))

    def a_far(zq, c):
        arrived(("far", c), gath.at[core, pl.ds(0, 3), zq, :, pl.ds(0, 32)])
        for d in (3, -3, 4):
            swap(rows_a(ring(y + d, NY), zq))

    def over_z(lo, zq, xq, group, arrivals):
        ref = rows_b(lo, 4, zq, xq)
        out(ref, group, arrivals[0], dz=1)
        out(ref, group, arrivals[1], dz=-1)
        out(rows_b(lo, 2, zq, xq), group, arrivals[2], dz=2)
        out(rows_b(lo + 2, 2, zq, xq), group, arrivals[2], dz=-2)

    def over_x(lo, zq, xq, group, arrivals):
        ref = rows_b(lo, 4, zq, xq)
        for d, name in zip((2, 1, 3), arrivals):
            out(ref, group, name, dx=d)

    z_from = (ring(zl - 1, NZ), ring(zl + 1, NZ), ring(zl + 2, NZ))
    x_from = (ring(x - 2, NX), ring(x - 1, NX), ring(x - 3, NX))

    own_a = rows_a(y, zl, x)
    own_b = gath.at[core, y, zl, x, pl.ds(32, 32)]
    own_c = gath.at[core, y, zl, x, pl.ds(64, 16)]
    for d in (2, 1, 3):
        out(own_a, "a1", "a1", dx=d)
    for d in (4, 3, 5, 2, 6, 1, 7):
        out(own_b, "b1", "b1", dy=d)
    for c in loads[1:8]:
        c.wait()
    ru = rk_up[...].astype(F32)
    top, bottom = ru[0:8], ru[8:16]
    odd = lax.rem(x, 2) == 1
    one = jnp.where(odd, bottom, top)
    two = jnp.where(odd, top, bottom)
    dn = down[...]
    zero = jnp.zeros_like(dn)
    wide = jnp.concatenate(
        [jnp.concatenate([dn, zero], axis=1), jnp.concatenate([zero, dn], axis=1)], axis=0
    )
    fold = nt(jnp.concatenate([one, two], axis=1).astype(BF), wide)
    aux_1 = jnp.concatenate([fold, up[...].astype(F32)], axis=0)
    wo = wout[...].astype(F32)
    aux_0 = jnp.concatenate([wo[:, :128], wo[:, 128:]], axis=0)
    first = core == 0
    gath[core, y, zl, x, 64:80, :] = jnp.where(first, aux_0, aux_1).astype(BF)
    for d in (4, 3, 5, 2, 6, 1, 7):
        out(own_c, "b1", "b1", dy=d)
    mask_rows()
    arrived("a1", gath.at[core, y, zl, pl.ds(0, 3), pl.ds(0, 32)])
    mine = rows_a(y, zl)
    out(mine, "a2", "a2-", dz=1)
    out(mine, "a2", "a2+", dz=-1)
    out(rows_a(y, zl, pl.ds(0, 2)), "a2", "a2=", dz=2)
    out(rows_a(y, zl, pl.ds(2, 2)), "a2", "a2=", dz=-2)
    a_plane(zl, 0)
    src, col = iota((512, 512), 0), iota((512, 512), 1)
    want = ((col >> 4) & 3) * 128 + ((col >> 2) & 3) * 32 + (col >> 6) * 4 + (col & 3)
    perm[...] = (src == want).astype(F32).astype(BF)
    arrived("b1", gath.at[core, pl.ds(0, 7), zl, x, pl.ds(32, 48)])
    over_z(0, zl, x, "b2", ("bx2-", "bx2+", "bx2="))
    over_x(4, zl, x, "b2", ("bz2a", "bz2b", "bz2c"))
    over_x(0, zl, x, "b3", (("bx3", 0),) * 3)
    over_z(4, zl, x, "b3", (("bz3", 0),) * 3)
    swap(rows_b(0, 8, zl, x))
    for c, name in enumerate(("a2-", "a2+", "a2=")):
        arrived(name, rows_a(y, z_from[c]))
        a_plane(z_from[c], c + 1)
    a_forward(zl, 0)
    a_near(zl, 0)

    def bx_next(c, name):
        zq = z_from[c]
        arrived(name, rows_b(0, 4, zq, x))
        over_x(0, zq, x, "b3", (("bx3", c + 1),) * 3)
        swap(rows_b(0, 4, zq, x))

    def bz_next(c, name):
        xq = x_from[c]
        arrived(name, rows_b(4, 4, zl, xq))
        over_z(4, zl, xq, "b3", (("bz3", c + 1),) * 3)
        swap(rows_b(4, 4, zl, xq))

    bx_next(0, "bx2-")
    bz_next(1, "bz2b")
    bx_next(1, "bx2+")
    bz_next(2, "bz2c")
    bz_next(0, "bz2a")
    bx_next(2, "bx2=")
    for c in range(3):
        a_forward(z_from[c], c + 1)
        a_near(z_from[c], c + 1)
    bz_order = (x, x_from[0], x_from[1], x_from[2])
    for c, zq in enumerate((zl,) + z_from):
        arrived(("bx3", c), gath.at[core, pl.ds(0, 4), zq, pl.ds(0, 3), pl.ds(32, 48)])
        for xq in x_from:
            swap(rows_b(0, 4, zq, xq))
        xq = bz_order[c]
        arrived(("bz3", c), gath.at[core, pl.ds(4, 4), pl.ds(0, 3), xq, pl.ds(32, 48)])
        for zr in z_from:
            swap(rows_b(4, 4, zr, xq))
        a_far(zq, c)
    loads[10].wait()
    loads[11].wait()
    arrived("swap", gath.at[1 - core])

    low = iota((8, 8, 128), 2) < 64

    def plane(k, acc):
        inward_c, inward_p, right_t, grad, outward = acc
        lanes = pl.ds(pl.multiple_of(k * 1024, 1024), 1024)
        xk = xs[:, lanes]
        w = jnp.concatenate(
            [gath[h, k, :, :, 0:64, :].reshape(1024, 128) for h in range(2)], axis=1
        )
        inward_c = inward_c + nn(xk[:128], w)
        inward_p = inward_p + nn(xk[128:], w)
        a0 = gath[0, k, :, :, 64:80, :].reshape(16, 16, 128).astype(F32)
        a1 = gath[1, k, :, :, 64:80, :].reshape(16, 16, 128).astype(F32)
        wo_k = jnp.concatenate(
            [a0[:, 0:8].reshape(128, 128), a0[:, 8:16].reshape(128, 128)], axis=1
        ).astype(BF)
        up_k = a1[:, 8:16].reshape(128, 128).astype(BF)
        pairs = a1[:, 0:8].reshape(8, 2, 8, 128)
        te, to = pairs[:, 0], pairs[:, 1]
        t8 = jnp.where(low, te, to)
        b8 = pltpu.roll(jnp.where(low, to, te), 64, 2)
        fold_t = jnp.concatenate(
            [jnp.concatenate([t8[m], b8[m]], axis=0) for m in range(8)], axis=1
        ).astype(BF)
        right_t = right_t + nt(fold_t, xk)
        mk = masked[:, pl.ds(pl.multiple_of(k * 128, 128), 128)]
        grad = grad + nn(mk, up_k)
        outward = outward + nn(mk, wo_k)
        return inward_c, inward_p, right_t, grad, outward

    zeros = lambda m, n: jnp.zeros((m, n), F32)
    inward_c, inward_p, right_t, grad, outward = lax.fori_loop(
        0, NY, plane, (zeros(128, 256), zeros(128, 256), zeros(16, 256), zeros(256, 128), zeros(256, 256))
    )

    own = lax.rem(iota((128, 256), 0), 8) == iota((128, 256), 1) // SEQ
    spread_k = one_hot_rows(128, 16, 8)
    rd = nn(spread_k, rk_down[...]).astype(BF)
    left_t = jnp.where(own, nt(rd, grad.astype(BF)), 0.0).astype(BF)
    right_t = jnp.where(own, nn(spread_k, right_t.astype(BF)), 0.0).astype(BF)
    gl = nn(left_t, jnp.concatenate([inward_c, inward_p], axis=0).astype(BF))
    gr = nn(right_t, outward.astype(BF))
    joined = jnp.concatenate(
        [g[8 * k : 8 * k + 8] for g in (gl, gr) for k in range(16)], axis=1
    )
    inv = lax.rsqrt(jnp.sum(joined * joined, axis=1, keepdims=True) / 8192.0 + EPS)
    normed = joined * inv
    feats[...] = normed.astype(BF)

    upper = iota((8, 512), 0) < 4
    for b in range(NY):
        lo = normed[:, 1024 * b : 1024 * b + 512]
        hi = normed[:, 1024 * b + 512 : 1024 * b + 1024]
        f_out[b] = jnp.where(upper, lo, pltpu.roll(hi, 4, 0)).astype(BF)
        p_out[b] = jnp.where(upper, pltpu.roll(lo, 4, 0), hi).astype(BF)
    for d in (4, 3, 5, 2, 6, 1, 7):
        to = lax.rem(y + d, NY)
        send(f_out.at[to], fblk.at[zl, y], at(dy=d), "feature", ("piece", d))
        send(p_out.at[to], pblk.at[x, y], at(dy=d), "feature", ("piece", d))
    fblk[zl, y] = f_out[y]
    pblk[x, y] = p_out[y]

    def pass_on(p):
        f, q = fblk.at[zl, p], pblk.at[x, p]
        for d in (3, 2, 1):
            send(f, f, at(z_in=lax.rem(zl + d, NZ)), "cands", "cands")
        for d in (2, 1, 3):
            send(q, q, at(dx=d), "probes", "probes")

    pass_on(y)
    for d in (1, 7, 2, 6, 3, 5, 4):
        arrived(("piece", d), f_out.at[pl.ds(0, 2)])
        pass_on(ring(y - d, NY))
    arrived("cands", fblk.at[pl.ds(0, 3)])
    arrived("probes", pblk.at[pl.ds(0, 3)])

    def halves(ref):
        lo, hi = [], []
        for k in range(4):
            for m in range(4):
                a, b = ref[k, 2 * m].astype(F32), ref[k, 2 * m + 1].astype(F32)
                lo.append(jnp.where(upper, a, pltpu.roll(b, 4, 0)))
                hi.append(jnp.where(upper, pltpu.roll(a, 4, 0), b))
        return tuple(jnp.concatenate(v, axis=0).astype(BF) for v in (lo, hi))

    f_lo, f_hi = halves(fblk)
    p_lo, p_hi = halves(pblk)
    prod = nt(f_lo, p_lo) + nt(f_hi, p_hi)

    upper = iota((8, 128), 0) < 4
    tile = lambda zq, m: prod[zq * 32 + m * 8 : zq * 32 + m * 8 + 8]
    for m in range(4):
        for h in range(2):
            a, b = tile(2 * h, m), tile(2 * h + 1, m)
            tsum[2 * m, 8 * h : 8 * h + 8] = jnp.where(upper, a, pltpu.roll(b, 4, 0))
            tsum[2 * m + 1, 8 * h : 8 * h + 8] = jnp.where(upper, pltpu.roll(a, 4, 0), b)
    tgot[y] = tsum[y]
    for d in (4, 3, 5, 2, 6, 1, 7):
        send(tsum.at[lax.rem(y + d, NY)], tgot.at[y], at(dy=d), "sums", "sums")
    arrived("sums", tgot.at[pl.ds(0, 7)])
    total = tgot[0]
    for k in range(1, NY):
        total = total + tgot[k]
    vsum[0] = total[0:8]
    vsum[1] = total[8:16]
    vgot[zl] = vsum[zl // 2]
    for d in range(1, NZ):
        tz = lax.rem(zl + d, NZ)
        send(vsum.at[tz // 2], vgot.at[zl], at(z_in=tz), "rows", "rows")
    arrived("rows", vgot.at[pl.ds(0, 3)])
    odd_z = lax.rem(zl, 2) == 1
    flat = jnp.concatenate(
        [jnp.where(odd_z, pltpu.roll(vgot[k], 4, 0), vgot[k]) for k in range(NZ)], axis=1
    )
    p1 = flat.astype(BF).astype(F32)
    p2 = (flat - p1).astype(BF).astype(F32)
    pieces = nn(jnp.concatenate([p1, p2, flat - p1 - p2], axis=0).astype(BF), perm[...])
    out_rows = pieces[0:8] + pieces[8:16] + pieces[16:24]
    scores[...] = out_rows * (1.0 / 8192.0)

    for group, ref in (
        ("a1", gath.at[core, y, zl, pl.ds(0, 3), pl.ds(0, 32)]),
        ("b1", gath.at[core, pl.ds(0, 7), zl, x, pl.ds(32, 48)]),
        ("a2", gath.at[core, y, pl.ds(0, 3), :, pl.ds(0, 32)]),
        ("plane", gath.at[core, pl.ds(0, 4), :, :, pl.ds(0, 32)]),
        ("forward", gath.at[core, pl.ds(0, 3), :, :, pl.ds(0, 32)]),
        ("b2", gath.at[core, pl.ds(0, 6), :, x, pl.ds(32, 48)]),
        ("b3", gath.at[core, pl.ds(0, 6), :, :, pl.ds(32, 48)]),
        ("swap", gath.at[core]),
        ("feature", fblk.at[pl.ds(0, 2), pl.ds(0, 7)]),
        ("cands", fblk.at[pl.ds(0, 3)]),
        ("probes", pblk.at[pl.ds(0, 3)]),
        ("sums", tsum.at[pl.ds(0, 7)]),
        ("rows", vgot.at[pl.ds(0, 3)]),
    ):
        left(group, ref)
    assert len(names["send"]) == N_SEND and len(names["recv"]) == N_RECV, names


def own_rows(scores, feats, own_scores, own_feats):
    own_scores[...] = scores[0:4]
    own_feats[...] = feats[0:4]


def body(xc, ct_c, len_c, xp, ct_p, len_p, down, up, win, wout, rk_down, rk_up):
    width, values = xc.shape[2], ct_c.shape[2]
    anyspace = pl.BlockSpec(memory_space=pl.ANY)
    vmem = pl.BlockSpec(memory_space=pltpu.VMEM)
    scores, feats = pl.pallas_call(
        kernel,
        out_shape=(
            jax.ShapeDtypeStruct((8, 512), F32),
            jax.ShapeDtypeStruct((8, 8192), BF),
        ),
        in_specs=[anyspace] * 12,
        out_specs=(vmem, vmem),
        scratch_shapes=[
            pltpu.SMEM((4,), jnp.int32),
            pltpu.SMEM((4,), jnp.int32),
            pltpu.VMEM((64, 128), BF),
            pltpu.VMEM((8, 128), BF),
            pltpu.VMEM((8, 256), BF),
            pltpu.VMEM((16, 128), BF),
            pltpu.VMEM((16, 128), BF),
            pltpu.VMEM((2, NY, NZ, NX, 80, 128), BF),
            pltpu.VMEM((256, 8192), BF),
            pltpu.VMEM((256, 1024), BF),
            pltpu.VMEM((256, 1024), BF),
            pltpu.VMEM((NY, 8, 512), BF),
            pltpu.VMEM((NY, 8, 512), BF),
            pltpu.VMEM((NZ, NY, 8, 512), BF),
            pltpu.VMEM((NX, NY, 8, 512), BF),
            pltpu.VMEM((NY, 16, 128), F32),
            pltpu.VMEM((NY, 16, 128), F32),
            pltpu.VMEM((2, 8, 128), F32),
            pltpu.VMEM((NZ, 8, 128), F32),
            pltpu.VMEM((512, 512), BF),
            pltpu.SemaphoreType.DMA((12,)),
            pltpu.SemaphoreType.DMA((N_SEND,)),
            pltpu.SemaphoreType.DMA((N_RECV,)),
        ],
        compiler_params=pltpu.CompilerParams(
            collective_id=0, has_side_effects=True, vmem_limit_bytes=67043328
        ),
        name="lora_scores",
    )(
        xc.reshape(-1, width), ct_c.reshape(-1, values), len_c,
        xp.reshape(-1, width), ct_p.reshape(-1, values), len_p,
        down, up, win, wout, rk_down.T, rk_up.T,
    )
    return pl.pallas_call(
        own_rows,
        out_shape=(
            jax.ShapeDtypeStruct((4, 512), F32),
            jax.ShapeDtypeStruct((4, 8192), BF),
        ),
        in_specs=[vmem, vmem],
        out_specs=(vmem, vmem),
        name="own_rows",
    )(scores, feats)


def solution(mesh):
    split = Mesh(mesh.devices.reshape(NY, NZ, NX, 2, 2), AXES)
    rows = P(FSDP, None)
    whole = P(DP_FSDP, None, None)
    return jax.shard_map(
        body,
        mesh=split,
        in_specs=(
            whole, whole, P(DP_FSDP), whole, whole, P(DP_FSDP), rows, rows, rows, rows, P(), P(),
        ),
        out_specs=(P(DP_FSDP, None), P(DP_FSDP, None)),
        check_vma=False,
    )
```

time: 69.4 us -> 62.7 us (0.903)
  Pallas kernels: 65.7 us -> 61.8 us
  local copies, waits for them, and re-layouts: 2.87 us -> 0 us
    pallas_call x1, Pallas kernels: 65.7 us -> 60.3 us  [body(): pl.pallas_call(kernel, out_shape=(jax.ShapeDtypeStruct((8, 512), F32), ja...]
    slice x2 -> x0, local copies, waits for them, and re-layouts: 2.87 us -> none  [body(): return (scores[:4], feats[:4])]
    pallas_call x0 -> x1, Pallas kernels: none -> 1.57 us  [body(): pl.pallas_call(own_rows, out_shape=(jax.ShapeDtypeStruct((4, 512), F32),...]
where the time goes in v3:
time: 62.7 us; the launch traced here: 62.5 us
  Pallas kernels  61.8 us (99%)
  between operations  0.64 us (1%)
    pallas_call x1, Pallas kernels, body(): pl.pallas_call(kernel, out_shape=(jax.ShapeDtypeStruct((8, 512), F32), ja...  60.3 us
    pallas_call x1, Pallas kernels, body(): pl.pallas_call(own_rows, out_shape=(jax.ShapeDtypeStruct((4, 512), F32),...  1.57 us

profile of v3, /device:TPU:8, one launch (start us, length us, event | category | flops | bytes accessed | tf_op | source)
XLA Modules:
  0.0 62.5 jit_solution(6815025179169612532)
XLA Ops:
  0.6 60.3 %lora_scores.1 = (f32[8,512]{1,0:T(8,128)}, bf16[8,8192]{1,0:T(8,128)(2,1)}) custom-call(bf16[128,8192]{1,0:T(8,128)(2,1)} %bitcast.6, bf16[128,1024]{1,0:T(8,128)(2,1)} %bitcast.8, s32[4]{0:T(128)} %len_ch.1, bf16[128,8192]{1,0:T(8,128)(2,1)} %bitcast.7, bf16[128,1024]{1,0:T(8,128)(2,1)} %bitcast.9, s32[4]{0:T(128)} %len_ph.1, bf16[64,128]{1,0:T(8,128)(2,1)} %down_h.1, ...), custom_call_target="tpu_custom_call" | custom-call | tf_op jit(solution)/shard_map/lora_scores/pallas_call | solution.py:412
  60.9 1.6 %own_rows.1 = (f32[4,512]{1,0:T(4,128)}, bf16[4,8192]{1,0:T(4,128)(2,1)}) custom-call(f32[8,512]{1,0:T(8,128)} %get-tuple-element.4.scores, bf16[8,8192]{1,0:T(8,128)(2,1)} %get-tuple-element.5.feats), custom_call_target="tpu_custom_call" | custom-call | tf_op jit(solution)/shard_map/own_rows/pallas_call | solution.py:454

commit v4 on v3

--- a/solution.py
+++ b/solution.py
@@ -37,7 +37,7 @@
     xc, ct_c, len_ch, xp, ct_p, len_ph, down_h, up_h, win_h, wout_h, rk_down_h, rk_up_h,
     scores, feats,
     len_c, len_p, down, up, wout, rk_down, rk_up,
-    gath, xs, cot, masked, f_out, p_out, fblk, pblk, tsum, tgot, vsum, vgot, perm,
+    gath, xs, cot, masked, f_out, p_out, fblk, pblk, tsum, tgot, vsum, vgot, perm, out_w, fold_w,
     ld_sem, send_sem, recv_sem,
 ):
     y, zl, x = (lax.axis_index(a) for a in FSDP)
@@ -192,10 +192,10 @@
     two = jnp.where(odd, top, bottom)
     dn = down[...]
     zero = jnp.zeros_like(dn)
-    wide = jnp.concatenate(
+    stacked = jnp.concatenate(
         [jnp.concatenate([dn, zero], axis=1), jnp.concatenate([zero, dn], axis=1)], axis=0
     )
-    fold = nt(jnp.concatenate([one, two], axis=1).astype(BF), wide)
+    fold = nt(jnp.concatenate([one, two], axis=1).astype(BF), stacked)
     aux_1 = jnp.concatenate([fold, up[...].astype(F32)], axis=0)
     wo = wout[...].astype(F32)
     aux_0 = jnp.concatenate([wo[:, :128], wo[:, 128:]], axis=0)
@@ -263,45 +263,41 @@
 
     low = iota((8, 8, 128), 2) < 64
 
-    def plane(k, acc):
-        inward_c, inward_p, right_t, grad, outward = acc
-        lanes = pl.ds(pl.multiple_of(k * 1024, 1024), 1024)
-        xk = xs[:, lanes]
-        w = jnp.concatenate(
-            [gath[h, k, :, :, 0:64, :].reshape(1024, 128) for h in range(2)], axis=1
-        )
-        inward_c = inward_c + nn(xk[:128], w)
-        inward_p = inward_p + nn(xk[128:], w)
+    def narrow(k, carry):
         a0 = gath[0, k, :, :, 64:80, :].reshape(16, 16, 128).astype(F32)
         a1 = gath[1, k, :, :, 64:80, :].reshape(16, 16, 128).astype(F32)
-        wo_k = jnp.concatenate(
-            [a0[:, 0:8].reshape(128, 128), a0[:, 8:16].reshape(128, 128)], axis=1
-        ).astype(BF)
-        up_k = a1[:, 8:16].reshape(128, 128).astype(BF)
+        rows = pl.ds(pl.multiple_of(k * 128, 128), 128)
+        out_w[rows, 0:128] = a0[:, 0:8].reshape(128, 128).astype(BF)
+        out_w[rows, 128:256] = a0[:, 8:16].reshape(128, 128).astype(BF)
+        out_w[rows, 256:384] = a1[:, 8:16].reshape(128, 128).astype(BF)
         pairs = a1[:, 0:8].reshape(8, 2, 8, 128)
         te, to = pairs[:, 0], pairs[:, 1]
         t8 = jnp.where(low, te, to)
         b8 = pltpu.roll(jnp.where(low, to, te), 64, 2)
-        fold_t = jnp.concatenate(
+        fold_w[:, pl.ds(pl.multiple_of(k * 1024, 1024), 1024)] = jnp.concatenate(
             [jnp.concatenate([t8[m], b8[m]], axis=0) for m in range(8)], axis=1
         ).astype(BF)
-        right_t = right_t + nt(fold_t, xk)
-        mk = masked[:, pl.ds(pl.multiple_of(k * 128, 128), 128)]
-        grad = grad + nn(mk, up_k)
-        outward = outward + nn(mk, wo_k)
-        return inward_c, inward_p, right_t, grad, outward
-
-    zeros = lambda m, n: jnp.zeros((m, n), F32)
-    inward_c, inward_p, right_t, grad, outward = lax.fori_loop(
-        0, NY, plane, (zeros(128, 256), zeros(128, 256), zeros(16, 256), zeros(256, 128), zeros(256, 256))
-    )
+        return carry
+
+    lax.fori_loop(0, NY, narrow, 0)
+    right_t = nt(fold_w[...], xs[...])
+    mixed = nn(masked[...], out_w[...])
+    outward, grad = mixed[:, :256], mixed[:, 256:]
+
+    def wide(h):
+        return jnp.concatenate(
+            [gath[h, k, :, :, 0:64, :].reshape(1024, 128) for k in range(NY)], axis=0
+        )
+
+    w = jnp.concatenate([wide(0), wide(1)], axis=1)
+    inward = nn(xs[...], w)
 
     own = lax.rem(iota((128, 256), 0), 8) == iota((128, 256), 1) // SEQ
     spread_k = one_hot_rows(128, 16, 8)
     rd = nn(spread_k, rk_down[...]).astype(BF)
     left_t = jnp.where(own, nt(rd, grad.astype(BF)), 0.0).astype(BF)
     right_t = jnp.where(own, nn(spread_k, right_t.astype(BF)), 0.0).astype(BF)
-    gl = nn(left_t, jnp.concatenate([inward_c, inward_p], axis=0).astype(BF))
+    gl = nn(left_t, inward.astype(BF))
     gr = nn(right_t, outward.astype(BF))
     joined = jnp.concatenate(
         [g[8 * k : 8 * k + 8] for g in (gl, gr) for k in range(16)], axis=1
@@ -438,6 +434,8 @@
             pltpu.VMEM((2, 8, 128), F32),
             pltpu.VMEM((NZ, 8, 128), F32),
             pltpu.VMEM((512, 512), BF),
+            pltpu.VMEM((1024, 384), BF),
+            pltpu.VMEM((16, 8192), BF),
             pltpu.SemaphoreType.DMA((12,)),
             pltpu.SemaphoreType.DMA((N_SEND,)),
             pltpu.SemaphoreType.DMA((N_RECV,)),

time: 62.7 us -> 61.6 us (0.982)
  Pallas kernels: 61.8 us -> 60.8 us
    pallas_call x1, Pallas kernels: 60.3 us -> 59.2 us  [body(): pl.pallas_call(kernel, out_shape=(jax.ShapeDtypeStruct((8, 512), F32), ja...]
where the time goes in v4:
time: 61.6 us; the launch traced here: 61.4 us
  Pallas kernels  60.8 us (99%)
  between operations  0.64 us (1%)
    pallas_call x1, Pallas kernels, body(): pl.pallas_call(kernel, out_shape=(jax.ShapeDtypeStruct((8, 512), F32), ja...  59.2 us
    pallas_call x1, Pallas kernels, body(): pl.pallas_call(own_rows, out_shape=(jax.ShapeDtypeStruct((4, 512), F32),...  1.57 us

profile of v4, /device:TPU:8, one launch (start us, length us, event | category | flops | bytes accessed | tf_op | source)
XLA Modules:
  0.0 61.4 jit_solution(16171191730850637709)
XLA Ops:
  0.6 59.2 %lora_scores.1 = (f32[8,512]{1,0:T(8,128)}, bf16[8,8192]{1,0:T(8,128)(2,1)}) custom-call(bf16[128,8192]{1,0:T(8,128)(2,1)} %bitcast.6, bf16[128,1024]{1,0:T(8,128)(2,1)} %bitcast.8, s32[4]{0:T(128)} %len_ch.1, bf16[128,8192]{1,0:T(8,128)(2,1)} %bitcast.7, bf16[128,1024]{1,0:T(8,128)(2,1)} %bitcast.9, s32[4]{0:T(128)} %len_ph.1, bf16[64,128]{1,0:T(8,128)(2,1)} %down_h.1, ...), custom_call_target="tpu_custom_call" | custom-call | tf_op jit(solution)/shard_map/lora_scores/pallas_call | solution.py:408
  59.8 1.6 %own_rows.1 = (f32[4,512]{1,0:T(4,128)}, bf16[4,8192]{1,0:T(4,128)(2,1)}) custom-call(f32[8,512]{1,0:T(8,128)} %get-tuple-element.4.scores, bf16[8,8192]{1,0:T(8,128)(2,1)} %get-tuple-element.5.feats), custom_call_target="tpu_custom_call" | custom-call | tf_op jit(solution)/shard_map/own_rows/pallas_call | solution.py:452

commit v5 on v4

--- a/solution.py
+++ b/solution.py
@@ -37,7 +37,7 @@
     xc, ct_c, len_ch, xp, ct_p, len_ph, down_h, up_h, win_h, wout_h, rk_down_h, rk_up_h,
     scores, feats,
     len_c, len_p, down, up, wout, rk_down, rk_up,
-    gath, xs, cot, masked, f_out, p_out, fblk, pblk, tsum, tgot, vsum, vgot, perm, out_w, fold_w,
+    gath, xs, cot, masked, f_out, p_out, fblk, pblk, tsum, tgot, vsum, vgot, perm, out_w, fold_w, f_rows,
     ld_sem, send_sem, recv_sem,
 ):
     y, zl, x = (lax.axis_index(a) for a in FSDP)
@@ -304,7 +304,9 @@
     )
     inv = lax.rsqrt(jnp.sum(joined * joined, axis=1, keepdims=True) / 8192.0 + EPS)
     normed = joined * inv
-    feats[...] = normed.astype(BF)
+    f_rows[...] = normed.astype(BF)
+    store = pltpu.make_async_copy(f_rows, feats, ld_sem.at[12])
+    store.start()
 
     upper = iota((8, 512), 0) < 4
     for b in range(NY):
@@ -377,6 +379,7 @@
     out_rows = pieces[0:8] + pieces[8:16] + pieces[16:24]
     scores[...] = out_rows * (1.0 / 8192.0)
 
+    store.wait()
     for group, ref in (
         ("a1", gath.at[core, y, zl, pl.ds(0, 3), pl.ds(0, 32)]),
         ("b1", gath.at[core, pl.ds(0, 7), zl, x, pl.ds(32, 48)]),
@@ -412,7 +415,7 @@
             jax.ShapeDtypeStruct((8, 8192), BF),
         ),
         in_specs=[anyspace] * 12,
-        out_specs=(vmem, vmem),
+        out_specs=(vmem, anyspace),
         scratch_shapes=[
             pltpu.SMEM((4,), jnp.int32),
             pltpu.SMEM((4,), jnp.int32),
@@ -436,7 +439,8 @@
             pltpu.VMEM((512, 512), BF),
             pltpu.VMEM((1024, 384), BF),
             pltpu.VMEM((16, 8192), BF),
-            pltpu.SemaphoreType.DMA((12,)),
+            pltpu.VMEM((8, 8192), BF),
+            pltpu.SemaphoreType.DMA((13,)),
             pltpu.SemaphoreType.DMA((N_SEND,)),
             pltpu.SemaphoreType.DMA((N_RECV,)),
         ],

time: 61.6 us -> 61.6 us (level)
  no operation moved by 1% of the time
where the time goes in v5:
time: 61.6 us; the launch traced here: 61.4 us
  Pallas kernels  60.7 us (99%)
  between operations  0.64 us (1%)
    pallas_call x1, Pallas kernels, body(): pl.pallas_call(kernel, out_shape=(jax.ShapeDtypeStruct((8, 512), F32), ja...  59.2 us
    pallas_call x1, Pallas kernels, body(): pl.pallas_call(own_rows, out_shape=(jax.ShapeDtypeStruct((4, 512), F32),...  1.57 us

profile of v5, /device:TPU:8, one launch (start us, length us, event | category | flops | bytes accessed | tf_op | source)
XLA Modules:
  0.0 61.4 jit_solution(15765599070302503819)
XLA Ops:
  0.6 59.2 %lora_scores.1 = (f32[8,512]{1,0:T(8,128)}, bf16[8,8192]{1,0:T(8,128)(2,1)}) custom-call(bf16[128,8192]{1,0:T(8,128)(2,1)} %bitcast.6, bf16[128,1024]{1,0:T(8,128)(2,1)} %bitcast.8, s32[4]{0:T(128)} %len_ch.1, bf16[128,8192]{1,0:T(8,128)(2,1)} %bitcast.7, bf16[128,1024]{1,0:T(8,128)(2,1)} %bitcast.9, s32[4]{0:T(128)} %len_ph.1, bf16[64,128]{1,0:T(8,128)(2,1)} %down_h.1, ...), custom_call_target="tpu_custom_call" | custom-call | tf_op jit(solution)/shard_map/lora_scores/pallas_call | solution.py:411
  59.8 1.6 %own_rows.1 = (f32[4,512]{1,0:T(4,128)}, bf16[4,8192]{1,0:T(4,128)(2,1)}) custom-call(f32[8,512]{1,0:T(8,128)} %get-tuple-element.4.scores, bf16[8,8192]{1,0:T(8,128)(2,1)} %get-tuple-element.5.feats), custom_call_target="tpu_custom_call" | custom-call | tf_op jit(solution)/shard_map/own_rows/pallas_call | solution.py:456
